TPU v7x, 32 devices: a whole 2x2x4 slice. The times are simulated.
32 devices in a mesh: scen: 16 (over z, y, core), net: 2 (over x).
Axes of the slice: x: 2, y: 2, z: 4, core: 2. Of those that a mesh axis runs over, the one named last changes fastest.
Arguments:
- generation: float32 [16, 168, 4096], P('scen', None, 'net'), may hold values from 0 to 2
- charging: float32 [16, 168, 1024], P('scen', None, 'net'), may hold values from 0 to 0.5
- discharging: float32 [16, 168, 1024], P('scen', None, 'net'), may hold values from 0 to 0.5
- plant_capacity: float32 [4096], P('net'), may hold values from 1 to 3
- store_capacity: float32 [1024], P('net'), may hold values from 4 to 12
- dual_balance: float32 [16, 168], P('scen'), may hold values from -6 to 6
- dual_line: float32 [16, 168, 8192], P('scen', None, 'net'), may hold values from -6 to 6
- dual_headroom: float32 [16, 168, 4096], P('scen', None, 'net'), may hold values from 0 to 1
- dual_empty: float32 [16, 168, 1024], P('scen', None, 'net'), may hold values from -1 to 0
- dual_full: float32 [16, 168, 1024], P('scen', None, 'net'), may hold values from 0 to 1
- availability: float32 [16, 168, 4096], P('scen', None, 'net'), may hold values from 0.1 to 1
- demand: float32 [16, 168], P('scen'), may hold values from 0.5 to 1.5
- line_base: float32 [16, 168, 8192], P('scen', None, 'net'), may hold values from -6 to 6
- line_limit: float32 [8192], P('net'), may hold values from 0.5 to 2
- fuel_cost: float32 [4096], P('net'), may hold values from 0.1 to 2
- plant_cost: float32 [4096], P('net'), may hold values from 0.1 to 1
- store_cost: float32 [1024], P('net'), may hold values from 0.05 to 0.5
- self_loss: float32 [1024], P('net'), may hold values from 0.002 to 0.05
- power_limit: float32 [1024], P('net'), may hold values from 0.5 to 2
- store_node: int32 [1024], P('net'), may hold values from 0 to 4095, as said below
- line_factors: float32 [16, 512, 10, 256], P('net', 'scen'), may hold values from -0.125 to 0.125
- block_pattern: int32 [16, 10], P('net'), may hold values from 0 to 15, as said below
Outputs:
- next_generation: float32 [16, 168, 4096], P('scen', None, 'net')
- next_charging: float32 [16, 168, 1024], P('scen', None, 'net')
- next_discharging: float32 [16, 168, 1024], P('scen', None, 'net')
- next_plant: float32 [4096], P('net')
- next_store: float32 [1024], P('net')
- next_balance: float32 [16, 168], P('scen')
- next_line: float32 [16, 168, 8192], P('scen', None, 'net')
- next_headroom: float32 [16, 168, 4096], P('scen', None, 'net')
- next_empty: float32 [16, 168, 1024], P('scen', None, 'net')
- next_full: float32 [16, 168, 1024], P('scen', None, 'net')
Inputs may be any that keep to these rules, and one draw needn't show every extreme that they name: `store_node`: storage unit k sits at a node of block k // 64. `block_pattern`: row b lists 10 different node blocks, the first of them b itself.
All inputs are finite; a program needn't handle non-finite values.
Results may differ from a plain program's by a relative error of at most 0.00016.
Values sent between devices are 32-bit elements; how exact they have to be, the bound alone decides.
A program may use at most 128 MiB of HBM per device.

v0:
```python
import functools

import jax
import jax.numpy as jnp
from jax import lax
from jax.experimental import pallas as pl
from jax.experimental.pallas import tpu as pltpu
from jax.sharding import PartitionSpec as P

LANES = 128
primal_step = 0.5
dual_step = 0.5
store_step = 0.05
level_step = 0.05
efficiency = 0.92
f32 = jnp.float32
bf16 = jnp.bfloat16
VMEM_BYTES = 56 * 1024 * 1024


def split(x):
    hi = x.astype(bf16)
    return hi, (x - hi.astype(f32)).astype(bf16)


def stacked(x):
    return jnp.concatenate([x, x - x.astype(bf16).astype(f32)], axis=0).astype(bf16)


def dot(a, b):
    return jnp.dot(a, b, preferred_element_type=f32)


def dot_t(a, b):
    return lax.dot_general(a, b, (((1,), (1,)), ((), ())), preferred_element_type=f32)


def slot_steps(slots):
    return [range(j, min(j + 2, slots)) for j in range(0, slots, 2)]


def image_kernel(slots, parts, pat, dual, fac, *refs):
    outs, acc = refs[-1 - parts : -1], refs[-1]
    g = pl.program_id(0)
    hours = dual.shape[0]
    lines = fac.shape[0] * fac.shape[2]

    @pl.when(g == 0)
    def _():
        acc[...] = jnp.zeros_like(acc)

    both = stacked(dual[...])
    hi = dual[...].astype(bf16)
    for js in slot_steps(slots):
        w = fac[:, 0, :, js[0] * LANES : (js[-1] + 1) * LANES].reshape(lines, len(js) * LANES)
        wh, wl = split(w)
        r = dot(both, wh)
        r = r[:hours] + r[hours:] + dot(hi, wl)
        for i, j in enumerate(js):
            b = pat[g, j]
            acc[b] = acc[b] + r[:, i * LANES : (i + 1) * LANES]

    @pl.when(g == pl.num_programs(0) - 1)
    def _():
        own = outs[0].shape[0]
        for s in range(parts):
            outs[s][...] = acc[s * own : (s + 1) * own]


def image_parts(pattern, dual, fac, parts, after):
    groups, slots = pattern.shape
    hours = dual.shape[0]
    scen, _, lines_local, width = fac.shape
    lines = scen * lines_local
    full = jax.ShapeDtypeStruct((groups, hours, LANES), f32)
    whole = pl.BlockSpec((groups, hours, LANES), lambda g, pat: (0, 0, 0))
    return pl.pallas_call(
        functools.partial(image_kernel, slots, parts),
        out_shape=[full] * parts,
        grid_spec=pltpu.PrefetchScalarGridSpec(
            num_scalar_prefetch=1,
            grid=(groups,),
            in_specs=[
                pl.BlockSpec((hours, lines), lambda g, pat: (0, g)),
                pl.BlockSpec((scen, 1, lines_local, width), lambda g, pat: (0, g, 0, 0)),
            ]
            + [pl.BlockSpec(memory_space=pl.ANY)] * len(after),
            out_specs=[whole] * parts,
            scratch_shapes=[pltpu.VMEM((groups * parts, hours, LANES), f32)],
        ),
        compiler_params=pltpu.CompilerParams(vmem_limit_bytes=VMEM_BYTES),
        cost_estimate=pl.CostEstimate(
            flops=6 * groups * hours * lines * width,
            bytes_accessed=4 * groups * lines * width,
            transcendentals=0,
        ),
        name="image",
    )(pattern, dual, fac, *after)


def flow_kernel(slots, parts, first, last, pat, fac, *refs):
    injs, refs = refs[:parts], refs[parts:]
    if not first:
        prev, refs = refs[0], refs[1:]
    if last:
        dual, base, limit = refs[:3]
        refs = refs[3:]
    out, total, held = refs
    g = pl.program_id(0)
    own, hours, _ = injs[0].shape
    lines = fac.shape[0] * fac.shape[2]

    @pl.when(g == 0)
    def _():
        rows = jnp.zeros((hours, LANES), f32)
        for s in range(parts):
            for b in range(own):
                x = injs[s][b]
                held[s * own + b] = stacked(x)
                rows = rows + x
        total[...] = rows

    flows = jnp.zeros((hours, lines), f32) if first else prev[...]
    for js in [range(slots)]:
        w = fac[:, 0, :, js[0] * LANES : (js[-1] + 1) * LANES].reshape(lines, len(js) * LANES)
        wh, wl = split(w)
        both = jnp.concatenate([held[pat[g, j]] for j in js], axis=1)
        hi = jnp.concatenate([held[pat[g, j], :hours] for j in js], axis=1)
        r = dot_t(both, wh)
        flows = flows + (r[:hours] + r[hours:] + dot_t(hi, wl))
    if last:
        moved = dual[...] + dual_step * flows
        low = -limit[...] - base[...]
        high = limit[...] - base[...]
        out[...] = moved - dual_step * jnp.minimum(jnp.maximum(moved / dual_step, low), high)
    else:
        out[...] = flows


def flow_step(pattern, fac, injs, prev, tail):
    groups, slots = pattern.shape
    parts = len(injs)
    hours = injs[0].shape[1]
    scen, _, lines_local, width = fac.shape
    lines = scen * lines_local
    by_group = pl.BlockSpec((hours, lines), lambda g, pat: (0, g))
    whole = pl.BlockSpec((groups, hours, LANES), lambda g, pat: (0, 0, 0))
    operands = list(injs)
    specs = [whole] * parts
    if prev is not None:
        operands.append(prev)
        specs.append(by_group)
    if tail is not None:
        operands += list(tail)
        specs += [by_group, by_group, pl.BlockSpec((1, lines), lambda g, pat: (0, g))]
    return pl.pallas_call(
        functools.partial(flow_kernel, slots, parts, prev is None, tail is not None),
        out_shape=[
            jax.ShapeDtypeStruct((hours, groups * lines), f32),
            jax.ShapeDtypeStruct((hours, LANES), f32),
        ],
        grid_spec=pltpu.PrefetchScalarGridSpec(
            num_scalar_prefetch=1,
            grid=(groups,),
            in_specs=[
                pl.BlockSpec((scen, 1, lines_local, width), lambda g, pat: (0, g, 0, 0)),
            ]
            + specs,
            out_specs=[by_group, pl.BlockSpec((hours, LANES), lambda g, pat: (0, 0))],
            scratch_shapes=[pltpu.VMEM((groups * parts, 2 * hours, LANES), bf16)],
        ),
        compiler_params=pltpu.CompilerParams(vmem_limit_bytes=VMEM_BYTES),
        cost_estimate=pl.CostEstimate(
            flops=6 * groups * hours * lines * width,
            bytes_accessed=4 * groups * lines * width,
            transcendentals=0,
        ),
        name="flows",
    )(pattern, fac, *operands)


def decayed_sums(x, keep, reverse):
    hours = x.shape[0]
    hour = lax.broadcasted_iota(jnp.int32, x.shape, 0)
    power = keep
    lag = 1
    while lag < hours:
        if reverse:
            moved = jnp.where(hour < hours - lag, pltpu.roll(x, hours - lag, 0), 0.0)
        else:
            moved = jnp.where(hour >= lag, pltpu.roll(x, lag, 0), 0.0)
        x = x + power * moved
        power = power * power
        lag *= 2
    return x


def adjoint_kernel(empty, full, loss, out):
    out[...] = decayed_sums(empty[...] + full[...], 1.0 - loss[...], True)


def level_kernel(charging, discharging, next_c, next_d, empty, full, loss, extra, out_e, out_f):
    extra_c = 2.0 * next_c[...] - charging[...]
    extra_d = 2.0 * next_d[...] - discharging[...]
    drive = efficiency * extra_c - extra_d / efficiency
    levels = decayed_sums(drive, 1.0 - loss[...], False)
    out_e[...] = jnp.minimum(empty[...] + level_step * levels, 0.0)
    out_f[...] = jnp.maximum(full[...] + level_step * (levels - extra[...]), 0.0)


def simple_call(kernel, out_shape, name, *operands):
    moved = sum(4 * x.size for x in operands) + sum(
        4 * x.size for x in jax.tree.leaves(out_shape)
    )
    return pl.pallas_call(
        kernel,
        out_shape=out_shape,
        compiler_params=pltpu.CompilerParams(vmem_limit_bytes=VMEM_BYTES),
        cost_estimate=pl.CostEstimate(flops=8 * moved, bytes_accessed=moved, transcendentals=0),
        name=name,
    )(*operands)


def dispatch_kernel(chunk, width, parts, store_blk, *refs):
    images, refs = refs[:parts], refs[parts:]
    (balance, generation, headroom, fuel, charging, discharging, backward, power, rows,
     price_in, gen_in, gen_out, inj, price_out, out_c, out_d) = refs
    groups = images[0].shape[0]
    per = LANES // store_blk
    gen_out[...] = gen_in[...]
    for t in range(groups // per):
        prices, extras = [], []
        for b in range(t * per, (t + 1) * per):
            cols = slice(b * width + chunk * LANES, b * width + (chunk + 1) * LANES)
            image = images[0][b]
            for other in images[1:]:
                image = image + other[b]
            price = balance[...] + image
            gen = generation[:, cols]
            moved = jnp.maximum(gen - primal_step * (fuel[:, cols] + price + headroom[:, cols]), 0.0)
            gen_out[:, cols] = moved
            prices.append(price)
            extras.append(2.0 * moved - gen)
        units = slice(t * LANES, (t + 1) * LANES)
        place = lax.broadcasted_iota(jnp.int32, (per * LANES, LANES), 0)
        marks = jnp.where(place == rows[:, units], 1.0, 0.0).astype(bf16)
        hi, lo = split(jnp.concatenate(prices, axis=1))
        price = price_in[:, units] + (dot(hi, marks) + dot(lo, marks))
        price_out[:, units] = price
        back = backward[:, units]
        cap = power[:, units]
        c, d = charging[:, units], discharging[:, units]
        next_c = jnp.minimum(jnp.maximum(c - store_step * (efficiency * back - price), 0.0), cap)
        next_d = jnp.minimum(jnp.maximum(d - store_step * (price - back / efficiency), 0.0), cap)
        out_c[:, units] = next_c
        out_d[:, units] = next_d
        hi, lo = split((2.0 * next_d - d) - (2.0 * next_c - c))
        spread = dot_t(hi, marks) + dot_t(lo, marks)
        for i in range(per):
            inj[t * per + i] = extras[i] + spread[:, i * LANES : (i + 1) * LANES]


def body(
    generation, charging, discharging, plant_capacity, store_capacity, dual_balance, dual_line,
    dual_headroom, dual_empty, dual_full, availability, demand, line_base, line_limit, fuel_cost,
    plant_cost, store_cost, self_loss, power_limit, store_node, line_factors, block_pattern,
):
    scen_rows, hours, node_local = generation.shape
    groups, lines_local, slots, width = line_factors.shape
    parts = lax.axis_size("net")
    scen_size = lax.axis_size("scen")
    block_count = groups * parts
    stores = store_node.shape[0]
    store_blk = stores // groups
    chunks = width // LANES
    me = lax.axis_index("net")

    gen, chg, dis = generation[0], charging[0], discharging[0]
    line, head = dual_line[0], dual_headroom[0]
    empty, full, avail = dual_empty[0], dual_full[0], availability[0]
    loss = self_loss[None, :]

    pattern = (block_pattern - me * groups + block_count) % block_count
    node = store_node - me * node_local
    unit = jnp.arange(stores, dtype=jnp.int32)
    per = LANES // store_blk
    pair_row = (node // width - (unit // LANES) * per) * LANES + node % LANES
    gathered = []
    for q in range(chunks):
        piece = line_factors[:, :, :, q * LANES : (q + 1) * LANES]
        piece = piece.reshape(groups, lines_local, slots * LANES)
        gathered.append(lax.all_gather(piece, "scen", axis=0))

    backward = simple_call(
        adjoint_kernel, jax.ShapeDtypeStruct((hours, stores), f32), "adjoint", empty, full, loss
    )
    plant_part = jnp.sum(avail * head, axis=0)
    store_part = jnp.sum(full, axis=0)
    totals = lax.psum(jnp.concatenate([plant_part, store_part]), "scen")
    plant_total, store_total = totals[:node_local], totals[node_local:]
    scen_hours = scen_rows * scen_size * hours
    next_plant = jnp.maximum(
        plant_capacity - primal_step * (plant_cost - plant_total / scen_hours), 0.0
    )
    next_store = jnp.maximum(
        store_capacity - primal_step * (store_cost - store_total / scen_hours), 0.0
    )
    extra_plant = 2.0 * next_plant - plant_capacity
    extra_store = 2.0 * next_store - store_capacity

    price = jnp.zeros((hours, stores), f32)
    next_gen = gen
    flows = None
    totals_by_lane = jnp.zeros((hours, LANES), f32)
    by_store = jax.ShapeDtypeStruct((hours, stores), f32)
    by_node = jax.ShapeDtypeStruct((hours, node_local), f32)
    for q in range(chunks):
        after = [totals, backward] if q == 0 else [flows]
        partial_images = image_parts(pattern, line, gathered[q], parts, after)
        images = [partial_images[0]]
        for s in range(1, parts):
            images.append(
                lax.ppermute(partial_images[s], "net", [(i, (i + s) % parts) for i in range(parts)])
            )
        rows = jnp.where((node % width) // LANES == q, pair_row, -1)[None, :]
        next_gen, inj, price, next_c, next_d = simple_call(
            functools.partial(dispatch_kernel, q, width, parts, store_blk),
            [by_node, jax.ShapeDtypeStruct((groups, hours, LANES), f32), by_store, by_store, by_store],
            "dispatch",
            *images, dual_balance[0][:, None], gen, head, fuel_cost[None, :], chg, dis, backward,
            power_limit[None, :], rows, price, next_gen,
        )
        injs = [inj]
        for s in range(1, parts):
            injs.append(lax.ppermute(inj, "net", [(i, (i - s) % parts) for i in range(parts)]))
        tail = (line, line_base[0], line_limit[None, :]) if q == chunks - 1 else None
        flows, sums = flow_step(pattern, gathered[q], injs, flows, tail)
        totals_by_lane = totals_by_lane + sums

    next_empty, next_full = simple_call(
        level_kernel, [by_store, by_store], "levels",
        chg, dis, next_c, next_d, empty, full, loss, extra_store[None, :],
    )
    extra_generation = 2.0 * next_gen - gen
    next_headroom = jnp.maximum(head + dual_step * (extra_generation - avail * extra_plant), 0.0)
    next_balance = dual_balance + dual_step * (
        jnp.sum(totals_by_lane, axis=1)[None] / (block_count * width) - demand
    )
    return (
        next_gen[None], next_c[None], next_d[None], next_plant, next_store, next_balance,
        flows[None], next_headroom[None], next_empty[None], next_full[None],
    )


def solution(mesh):
    row = P("scen", None, "net")
    placed = (
        row, row, row, P("net"), P("net"), P("scen", None), row, row, row, row, row,
        P("scen", None), row, P("net"), P("net"), P("net"), P("net"), P("net"), P("net"), P("net"),
        P("net", "scen", None, None), P("net", None),
    )
    return jax.shard_map(
        body,
        mesh=mesh,
        in_specs=placed,
        out_specs=(row, row, row, P("net"), P("net"), P("scen", None), row, row, row, row),
        check_vma=False,
    )
```

profile of v0, /device:TPU:0, one launch (start us, length us, event | category | flops | bytes accessed | tf_op | source)
XLA Modules:
  0.0 317.8 jit_solution(13198479756610399380)
XLA Ops:
  7.2 0.0 all-gather.5.cloned.1.call-start
  7.2 2.0 fusion.29
  9.2 0.8 copy.39
  10.0 1.3 all_gather_reshape.7
  11.3 0.0 all-gather.5.cloned.1.call-update
  11.4 0.0 all-gather.3.cloned.1.call-start
  11.4 0.8 copy.38
  12.2 0.0 copy-start.3
  12.2 1.3 all_gather_reshape.6
  13.5 0.0 all-gather.3.cloned.1.call-update
  13.5 1.1 reduce_sum.28
  14.7 2.1 adjoint.1.refs_1_.refs_8_
  16.8 0.0 copy-done.3
  16.8 0.2 fusion
  17.0 64.6 %psum.7.refs_0_ = f32[2560]{0:T(1024)} all-reduce(f32[2560]{0:T(1024)S(1)} %pad_maximum_fusion), channel_id=1, replica_groups=mesh['scen'=16,'net'=2] {'scen'}, use_global_device_ids=true, to_apply=%region_2.3 | all-reduce | flops 2560 | bytes 20480 | tf_op jit(solution)/shard_map/psum | solution.py:299
  81.6 0.0 copy-done.13
  81.6 0.6 add_select_fusion.pat
  82.2 42.0 %all-gather.5.cloned.1.call-done.fac = f32[16,8,32,1280]{3,2,1,0:T(8,128)} async-done(((f32[1,8,32,1280]{3,2,1,0:T(8,128)}), f32[16,8,32,1280]{3,2,1,0:T(8,128)}) %all-gather.5.cloned.1.call-update) | async-done | bytes 20971536 | tf_op jit(solution)/shard_map/all_gather | solution.py:292
  124.1 15.2 %image.2 = (f32[8,168,128]{2,1,0:T(8,128)}, f32[8,168,128]{2,1,0:T(8,128)}) custom-call(s32[8,10]{1,0:T(8,128)} %add_select_fusion.pat, f32[168,4096]{1,0:T(8,128)} %bitcast.43, f32[16,8,32,1280]{3,2,1,0:T(8,128)} %all-gather.5.cloned.1.call-done.fac, f32[2560]{0:T(1024)} %psum.7.refs_0_, f32[168,512]{1,0:T(8,128)} %adjoint.1.refs_1_.refs_8_), custom_call_target="tpu_custom_call" | custom-call | flops 5284823040 | bytes 20971520 | tf_op jit(solution)/shard_map/image/pallas_call | solution.py:77
  139.4 1.2 collective-permute-start
  140.6 0.0 copy-done.12
  140.6 0.8 copy.40.refs_2_
  141.3 0.6 compare_select_fusion
  141.9 0.6 compare_select_fusion.1
  142.5 14.6 %collective-permute-done.refs_1_ = f32[8,168,128]{2,1,0:T(8,128)S(1)} collective-permute-done((f32[8,168,128]{2,1,0:T(8,128)}, f32[8,168,128]{2,1,0:T(8,128)S(1)}, u32[]{:S(2)}, u32[]{:S(2)}) %collective-permute-start) | collective-permute-done | bytes 688160 | tf_op jit(solution)/shard_map/ppermute | solution.py:323
  157.1 0.8 broadcast_in_dim.56.refs_11_
  158.0 0.1 copy-done.6
  158.1 5.6 %dispatch.2 = (f32[168,2048]{1,0:T(8,128)}, f32[8,168,128]{2,1,0:T(8,128)}, f32[168,512]{1,0:T(8,128)}, f32[168,512]{1,0:T(8,128)}, f32[168,512]{1,0:T(8,128)}) custom-call(f32[8,168,128]{2,1,0:T(8,128)} %get-tuple-element.27.refs_0_, f32[8,168,128]{2,1,0:T(8,128)} %copy-done.6, f32[168,1]{1,0:T(8,128)} %copy.40.refs_2_, f32[168,2048]{1,0:T(8,128)} %bitcast.48, ...), custom_call_target="tpu_custom_call" | custom-call | flops 79926528 | bytes 9990816 | tf_op jit(solution)/shard_map/dispatch/pallas_call | solution.py:215
  163.7 1.3 collective-permute-start.1
  165.0 15.7 %collective-permute-done.1.refs_1_ = f32[8,168,128]{2,1,0:T(8,128)S(1)} collective-permute-done((f32[8,168,128]{2,1,0:T(8,128)}, f32[8,168,128]{2,1,0:T(8,128)S(1)}, u32[]{:S(2)}, u32[]{:S(2)}) %collective-permute-start.1) | collective-permute-done | bytes 688160 | tf_op jit(solution)/shard_map/ppermute | solution.py:335
  180.7 0.8 copy-done.5
  181.6 15.4 %flows.2 = (f32[168,4096]{1,0:T(8,128)}, f32[168,128]{1,0:T(8,128)}) custom-call(s32[8,10]{1,0:T(8,128)} %add_select_fusion.pat, f32[16,8,32,1280]{3,2,1,0:T(8,128)} %all-gather.5.cloned.1.call-done.fac, f32[8,168,128]{2,1,0:T(8,128)} %get-tuple-element.29.refs_0_, f32[8,168,128]{2,1,0:T(8,128)} %copy-done.5), custom_call_target="tpu_custom_call" | custom-call | flops 5284823040 | bytes 20971520 | tf_op jit(solution)/shard_map/flows/pallas_call | solution.py:156
  197.0 38.4 %all-gather.3.cloned.1.call-done.fac = f32[16,8,32,1280]{3,2,1,0:T(8,128)} async-done(((f32[1,8,32,1280]{3,2,1,0:T(8,128)}), f32[16,8,32,1280]{3,2,1,0:T(8,128)}) %all-gather.3.cloned.1.call-update) | async-done | bytes 20971536 | tf_op jit(solution)/shard_map/all_gather | solution.py:292
  235.4 14.8 %image.3 = (f32[8,168,128]{2,1,0:T(8,128)}, f32[8,168,128]{2,1,0:T(8,128)}) custom-call(s32[8,10]{1,0:T(8,128)} %add_select_fusion.pat, f32[168,4096]{1,0:T(8,128)} %bitcast.44, f32[16,8,32,1280]{3,2,1,0:T(8,128)} %all-gather.3.cloned.1.call-done.fac, f32[168,4096]{1,0:T(8,128)} %get-tuple-element.30.refs_0_.refs_2_), custom_call_target="tpu_custom_call" | custom-call | flops 5284823040 | bytes 20971520 | tf_op jit(solution)/shard_map/image/pallas_call | solution.py:77
  250.2 1.5 collective-permute-start.2
  251.7 0.6 multiply_subtract_fusion
  252.3 15.7 %collective-permute-done.2.refs_1_ = f32[8,168,128]{2,1,0:T(8,128)S(1)} collective-permute-done((f32[8,168,128]{2,1,0:T(8,128)}, f32[8,168,128]{2,1,0:T(8,128)S(1)}, u32[]{:S(2)}, u32[]{:S(2)}) %collective-permute-start.2) | collective-permute-done | bytes 688160 | tf_op jit(solution)/shard_map/ppermute | solution.py:323
  268.0 0.9 copy-done.7
  268.9 5.6 %dispatch.3 = (f32[168,2048]{1,0:T(8,128)}, f32[8,168,128]{2,1,0:T(8,128)}, f32[168,512]{1,0:T(8,128)}, f32[168,512]{1,0:T(8,128)}, f32[168,512]{1,0:T(8,128)}) custom-call(f32[8,168,128]{2,1,0:T(8,128)} %get-tuple-element.31.refs_0_, f32[8,168,128]{2,1,0:T(8,128)} %copy-done.7, f32[168,1]{1,0:T(8,128)} %copy.40.refs_2_, f32[168,2048]{1,0:T(8,128)} %bitcast.50, ...), custom_call_target="tpu_custom_call" | custom-call | flops 79926528 | bytes 9990816 | tf_op jit(solution)/shard_map/dispatch/pallas_call | solution.py:215
  274.5 1.6 collective-permute-start.3
  276.1 0.6 multiply_subtract_fusion.1
  276.6 2.8 levels.1
  279.4 2.9 fusion.5
  282.4 9.2 %collective-permute-done.3.refs_1_ = f32[8,168,128]{2,1,0:T(8,128)S(1)} collective-permute-done((f32[8,168,128]{2,1,0:T(8,128)}, f32[8,168,128]{2,1,0:T(8,128)S(1)}, u32[]{:S(2)}, u32[]{:S(2)}) %collective-permute-start.3) | collective-permute-done | bytes 688160 | tf_op jit(solution)/shard_map/ppermute | solution.py:335
  291.6 0.9 copy-done.4
  292.4 16.9 %flows.3 = (f32[168,4096]{1,0:T(8,128)}, f32[168,128]{1,0:T(8,128)}) custom-call(s32[8,10]{1,0:T(8,128)} %add_select_fusion.pat, f32[16,8,32,1280]{3,2,1,0:T(8,128)} %all-gather.3.cloned.1.call-done.fac, f32[8,168,128]{2,1,0:T(8,128)} %get-tuple-element.39.refs_0_, f32[8,168,128]{2,1,0:T(8,128)} %copy-done.4, f32[168,4096]{1,0:T(8,128)} %get-tuple-element.30.refs_0_.refs_2_, ...), custom_call_target="tpu_custom_call" | custom-call | flops 5284823040 | bytes 20971520 | tf_op jit(solution)/shard_map/flows/pallas_call | solution.py:156
  309.3 1.0 add_reduce_fusion
  310.4 0.6 multiply_add_fusion
  (30 shorter events, 0.1 us)
Async XLA Ops:
  7.2 117.0 %all-gather.5.cloned.1.call-start = ((), (), s32[]{:S(2)}) async-start(), calls=%async_computation.1 | async-start | bytes 22282240 | tf_op jit(solution)/shard_map/all_gather | solution.py:292
  11.4 224.0 %all-gather.3.cloned.1.call-start = ((), (), s32[]{:S(2)}) async-start(), calls=%async_computation | async-start | bytes 22282240 | tf_op jit(solution)/shard_map/all_gather | solution.py:292
  12.2 4.6 %copy-start.3 = (f32[1,168,2048]{2,1,0:T(8,128)S(1)}, f32[1,168,2048]{2,1,0:T(8,128)}, u32[]{:S(2)}) copy-start(f32[1,168,2048]{2,1,0:T(8,128)} %param.32) | copy-start | bytes 4128772
  13.5 3.3 %copy-start = (f32[1,168,2048]{2,1,0:T(8,128)S(1)}, f32[1,168,2048]{2,1,0:T(8,128)}, u32[]{:S(2)}) copy-start(f32[1,168,2048]{2,1,0:T(8,128)} %param.29) | copy-start | bytes 4128772
  16.8 64.8 %copy-start.13 = (s32[8,10]{1,0:T(8,128)S(1)}, s32[8,10]{1,0:T(8,128)}, u32[]{:S(2)}) copy-start(s32[8,10]{1,0:T(8,128)} %param.43) | copy-start | bytes 964
  124.1 16.5 %copy-start.12 = (f32[1,168]{1,0:T(1,128)S(1)}, f32[1,168]{1,0:T(1,128)}, u32[]{:S(2)}) copy-start(f32[1,168]{1,0:T(1,128)} %param.27) | copy-start | bytes 2020
  124.1 17.2 %copy-start.14 = (s32[512]{0:T(512)S(1)}, s32[512]{0:T(512)}, u32[]{:S(2)}) copy-start(s32[512]{0:T(512)} %param.41) | copy-start | bytes 6148
  139.4 17.8 %collective-permute-start = (f32[8,168,128]{2,1,0:T(8,128)}, f32[8,168,128]{2,1,0:T(8,128)S(1)}, u32[]{:S(2)}, u32[]{:S(2)}) collective-permute-start(f32[8,168,128]{2,1,0:T(8,128)} %get-tuple-element.28), channel_id=1, source_target_pairs={{0,1},{1,0},{2,3},{3,2},{4,5},{5,4},{6,7},{7,6},{8,9},{9,8},{10,11... | collective-permute-start | bytes 2064392 | tf_op jit(solution)/shard_map/ppermute | solution.py:323
  157.1 1.0 copy-start.6
  163.7 17.1 %collective-permute-start.1 = (f32[8,168,128]{2,1,0:T(8,128)}, f32[8,168,128]{2,1,0:T(8,128)S(1)}, u32[]{:S(2)}, u32[]{:S(2)}) collective-permute-start(f32[8,168,128]{2,1,0:T(8,128)} %get-tuple-element.29.refs_0_), channel_id=1, source_target_pairs={{0,1},{1,0},{2,3},{3,2},{4,5},{5,4},{6,7},{7,6},{8,9},{9,8},{10,11... | collective-permute-start | bytes 2064392 | tf_op jit(solution)/shard_map/ppermute | solution.py:335
  180.7 0.8 copy-start.5
  235.4 16.3 %copy-start.8 = (f32[2560]{0:T(1024)S(1)}, f32[2560]{0:T(1024)}, u32[]{:S(2)}) copy-start(f32[2560]{0:T(1024)} %psum.7.refs_0_) | copy-start | bytes 30724
  235.4 16.3 %copy-start.10 = (f32[2048]{0:T(1024)S(1)}, f32[2048]{0:T(1024)}, u32[]{:S(2)}) copy-start(f32[2048]{0:T(1024)} %param.25) | copy-start | bytes 24580
  235.4 16.3 %copy-start.11 = (f32[2048]{0:T(1024)S(1)}, f32[2048]{0:T(1024)}, u32[]{:S(2)}) copy-start(f32[2048]{0:T(1024)} %param.37) | copy-start | bytes 24580
  250.2 17.8 %collective-permute-start.2 = (f32[8,168,128]{2,1,0:T(8,128)}, f32[8,168,128]{2,1,0:T(8,128)S(1)}, u32[]{:S(2)}, u32[]{:S(2)}) collective-permute-start(f32[8,168,128]{2,1,0:T(8,128)} %get-tuple-element.32), channel_id=1, source_target_pairs={{0,1},{1,0},{2,3},{3,2},{4,5},{5,4},{6,7},{7,6},{8,9},{9,8},{10,11... | collective-permute-start | bytes 2064392 | tf_op jit(solution)/shard_map/ppermute | solution.py:323
  268.0 0.9 copy-start.7
  268.9 7.2 %copy-start.15 = (f32[512]{0:T(512)S(1)}, f32[512]{0:T(512)}, u32[]{:S(2)}) copy-start(f32[512]{0:T(512)} %param.26) | copy-start | bytes 6148
  268.9 7.2 %copy-start.16 = (f32[512]{0:T(512)S(1)}, f32[512]{0:T(512)}, u32[]{:S(2)}) copy-start(f32[512]{0:T(512)} %param.38) | copy-start | bytes 6148
  268.9 10.5 %copy-start.2 = (f32[1,168,2048]{2,1,0:T(8,128)S(1)}, f32[1,168,2048]{2,1,0:T(8,128)}, u32[]{:S(2)}) copy-start(f32[1,168,2048]{2,1,0:T(8,128)} %param.22) | copy-start | bytes 4128772
  274.5 4.9 %copy-start.1 = (f32[1,168,2048]{2,1,0:T(8,128)S(1)}, f32[1,168,2048]{2,1,0:T(8,128)}, u32[]{:S(2)}) copy-start(f32[1,168,2048]{2,1,0:T(8,128)} %param.29) | copy-start | bytes 4128772
  274.5 17.1 %collective-permute-start.3 = (f32[8,168,128]{2,1,0:T(8,128)}, f32[8,168,128]{2,1,0:T(8,128)S(1)}, u32[]{:S(2)}, u32[]{:S(2)}) collective-permute-start(f32[8,168,128]{2,1,0:T(8,128)} %get-tuple-element.39.refs_0_), channel_id=1, source_target_pairs={{0,1},{1,0},{2,3},{3,2},{4,5},{5,4},{6,7},{7,6},{8,9},{9,8},{10,11... | collective-permute-start | bytes 2064392 | tf_op jit(solution)/shard_map/ppermute | solution.py:335
  291.6 0.9 copy-start.4
  292.4 16.9 %copy-start.9 = (f32[168,128]{1,0:T(8,128)S(1)}, f32[168,128]{1,0:T(8,128)}, u32[]{:S(2)}) copy-start(f32[168,128]{1,0:T(8,128)} %get-tuple-element.38) | copy-start | bytes 258052
  292.4 17.9 %copy-start.17 = (f32[1,168]{1,0:T(1,128)S(1)}, f32[1,168]{1,0:T(1,128)}, u32[]{:S(2)}) copy-start(f32[1,168]{1,0:T(1,128)} %param.33) | copy-start | bytes 2020
Sparse Core Ops, SparseCore 0:
  11.5 112.6 all-gather.4
  126.3 109.0 all-gather.2
where the time goes:
time: 319 us; the launch traced here: 318 us
  waiting for transfers between devices  136 us (43%)
  Pallas kernels  78.4 us (25%)
  blocking collectives  64.6 us (20%)
  between operations  14.2 us (4%)
  local copies, waits for them, and re-layouts  10.5 us (3%)
  other arithmetic  8.78 us (3%)
  starting transfers between devices  5.67 us (2%)
    all_gather x2, waiting for transfers between devices, body(): gathered.append(lax.all_gather(piece, 'scen', axis=0))  80.4 us
    psum x1, blocking collectives, body(): totals = lax.psum(jnp.concatenate([plant_part, store_part]), 'scen')  64.6 us
    pallas_call x2, Pallas kernels, flow_step(): pl.pallas_call(functools.partial(flow_kernel, slots, parts, prev is None,...  32.3 us
    ppermute x2, waiting for transfers between devices, body(): lax.ppermute(partial_images[s], 'net', [(i, (i + s) % parts) for i in ran...  30.3 us
    pallas_call x2, Pallas kernels, image_parts(): pl.pallas_call(functools.partial(image_kernel, slots, parts), out_shape=[...  30 us
    ppermute x2, waiting for transfers between devices, body(): lax.ppermute(inj, 'net', [(i, (i - s) % parts) for i in range(parts)])  24.9 us
    pallas_call x4, Pallas kernels, simple_call(): pl.pallas_call(kernel, out_shape=out_shape, compiler_params=pltpu.Compile...  16.1 us
  transfers between devices with their start and end apart: 6, of which 6 were waited for; matrix products, arithmetic and copies ran while one was open for 3% of the time, Pallas kernels for 13%

commit v1 on v0

v1 whole, which is shorter than its diff:
```python
import functools

import jax
import jax.numpy as jnp
from jax import lax
from jax.experimental import pallas as pl
from jax.experimental.pallas import tpu as pltpu
from jax.sharding import PartitionSpec as P

LANES = 128
primal_step = 0.5
dual_step = 0.5
store_step = 0.05
level_step = 0.05
efficiency = 0.92
f32 = jnp.float32
bf16 = jnp.bfloat16
VMEM_BYTES = 56 * 1024 * 1024
MESH = pl.DeviceIdType.MESH
UP, DOWN, RIGHT, LEFT, CORE = range(5)


def split(x):
    hi = x.astype(bf16)
    return hi, (x - hi.astype(f32)).astype(bf16)


def stacked(x):
    return jnp.concatenate([x, x - x.astype(bf16).astype(f32)], axis=0).astype(bf16)


def dot(a, b):
    return jnp.dot(a, b, preferred_element_type=f32)


def dot_t(a, b):
    return lax.dot_general(a, b, (((1,), (1,)), ((), ())), preferred_element_type=f32)


def decayed_sums(x, keep, reverse):
    hours = x.shape[0]
    hour = lax.broadcasted_iota(jnp.int32, x.shape, 0)
    power = keep
    lag = 1
    while lag < hours:
        if reverse:
            moved = jnp.where(hour < hours - lag, pltpu.roll(x, hours - lag, 0), 0.0)
        else:
            moved = jnp.where(hour >= lag, pltpu.roll(x, lag, 0), 0.0)
        x = x + power * moved
        power = power * power
        lag *= 2
    return x


def when_all(conds, fn):
    if not conds:
        fn()
        return
    c = conds[0]
    for d in conds[1:]:
        c = jnp.logical_and(c, d)
    pl.when(c)(fn)


class Sizes:
    def __init__(self, scen, parts, generation, line_factors, store_node):
        _, self.hours, self.nodes = generation.shape
        self.groups, self.lines_local, self.slots, self.width = line_factors.shape
        self.scen, self.parts = scen, parts
        self.stores = store_node.shape[0]
        self.per = LANES // (self.stores // self.groups)
        assert self.per == 2
        self.cols = LANES // self.per
        self.chunks = self.width // self.cols
        self.pairs = -(-self.slots // self.per)
        self.wide = self.pairs * LANES
        self.lines = scen * self.lines_local
        self.rows = self.groups * self.lines_local
        self.blocks = self.groups * parts
        cut = -(-self.rows * 5 // 32 // 8) * 8
        self.cuts = ((0, self.rows - cut), (self.rows - cut, cut))
        plane = scen // 2
        self.rounds = scen.bit_length() - 1
        assert 2**self.rounds == scen
        self.b = max(d for d in range(1, plane + 1) if plane % d == 0 and d * d <= plane)
        self.a = plane // self.b


class Gather:
    def __init__(self, z, own, full, ssem, rsem):
        self.z, self.own, self.full, self.ssem, self.rsem = z, own, full, ssem, rsem
        self.me = lax.axis_index("scen")
        self.net = lax.axis_index("net")
        self.c = self.me % 2
        self.ib = (self.me // 2) % z.b
        self.ia = self.me // (2 * z.b)

    def slot(self, a, b):
        return (a * self.z.b + b) * 2 + self.c

    def has(self, way):
        return {
            UP: [self.ia < self.z.a - 1],
            DOWN: [self.ia > 0],
            RIGHT: [self.ib < self.z.b - 1],
            LEFT: [self.ib > 0],
            CORE: [],
        }[way]

    def device(self, way):
        z = self.z
        step = {UP: 2 * z.b, DOWN: -2 * z.b, RIGHT: 2, LEFT: -2}
        to = self.me + 1 - 2 * self.c if way == CORE else self.me + step[way]
        return (to, self.net)

    def copy(self, q, part, slot, way, own):
        start, size = self.z.cuts[part]
        rows = pl.ds(start, size)
        src = self.own.at[q, rows] if own else self.full.at[q, slot, rows]
        item = ((q * 2 + part) * (self.z.scen // 2) + slot // 2) * 5 + way
        return pltpu.make_async_remote_copy(
            src_ref=src,
            dst_ref=self.full.at[q, slot, rows],
            send_sem=self.ssem.at[item],
            recv_sem=self.rsem.at[(q * 2 + part) * self.z.scen + slot],
            device_id=self.device(way),
            device_id_type=MESH,
        )

    def arrivals(self):
        na, nb = self.z.a, self.z.b
        span = [0] + [s * k for k in range(1, na) for s in (-1, 1)]
        side = [0] + [s * k for k in range(1, nb) for s in (-1, 1)]
        steps = [[] for _ in range(na)]
        for t in range(na - 1):
            for s, way in ((-1, UP), (1, DOWN)):
                steps[t].append((0, s * (t + 1), 0, [way, RIGHT, LEFT, CORE]))
        for u in range(nb - 1):
            for s, way in ((-1, RIGHT), (1, LEFT)):
                steps[min(u, na - 1)].append((1, 0, s * (u + 1), [way, UP, DOWN, CORE]))
        for t in range(na - 1):
            for e in side:
                for s, way in ((-1, UP), (1, DOWN)):
                    steps[min(na - 1, t + max(abs(e) - 1, 0))].append((1, s * (t + 1), e, [way, CORE]))
        for u in range(nb - 1):
            for d in span:
                for s, way in ((-1, RIGHT), (1, LEFT)):
                    steps[min(na - 1, abs(d) + u)].append((0, d, s * (u + 1), [way, CORE]))
        return steps

    def valid(self, d, e):
        out = []
        if d < 0:
            out.append(self.ia + d >= 0)
        if d > 0:
            out.append(self.ia + d < self.z.a)
        if e < 0:
            out.append(self.ib + e >= 0)
        if e > 0:
            out.append(self.ib + e < self.z.b)
        return out

    def start_own(self, q):
        for part in range(2):
            for way in (UP, DOWN, RIGHT, LEFT, CORE):
                when_all(
                    self.has(way),
                    lambda: self.copy(q, part, self.me, way, True).start(),
                )

    def step(self, q, t):
        for part, d, e, ways in self.arrivals()[t]:
            def arrive(part=part, d=d, e=e, ways=ways):
                slot = self.slot(self.ia + d, self.ib + e)
                self.copy(q, part, slot, CORE, False).wait_recv()
                for way in ways:
                    when_all(
                        self.has(way),
                        lambda: self.copy(q, part, slot, way, False).start(),
                    )
            when_all(self.valid(d, e), arrive)

    def finish(self, q):
        def one(i, carry):
            for part in range(2):
                self.copy(q, part, 2 * i + 1 - self.c, CORE, False).wait_recv()
            return carry
        lax.fori_loop(0, self.z.scen // 2, one, 0)

    def drain(self, q):
        for part in range(2):
            for way in (UP, DOWN, RIGHT, LEFT, CORE):
                when_all(
                    self.has(way),
                    lambda: self.copy(q, part, self.me, way, True).wait_send(),
                )
        for step in self.arrivals():
            for part, d, e, ways in step:
                def sent(part=part, d=d, e=e, ways=ways):
                    slot = self.slot(self.ia + d, self.ib + e)
                    for way in ways:
                        when_all(
                            self.has(way),
                            lambda: self.copy(q, part, slot, way, False).wait_send(),
                        )
                when_all(self.valid(d, e), sent)


def step_kernel(
    z, pat, fac_h, line_h, base_h, gen_h, head_h, avail_h, chg_h, dis_h, empty_h, full_h,
    balance, demand, fuel, loss, power, node, limit, plant, plant_cost, stored, store_cost,
    full, gen_out, out_c, out_d, out_p, out_s, out_b, out_line, out_h, out_e, out_f,
    duals, wh, wl, fbuf, fac, own, parts_r, img, img_in, inj, inj_in, held,
    line, base, gen, head, avail, chg, dis, empty, dfull, back, price, place, total, sums, sums_in, tab,
    ssem, rsem, fsem, xsem, msem, tsem,
):
    me, net = lax.axis_index("scen"), lax.axis_index("net")
    half = z.groups // z.per
    lane = lax.broadcasted_iota(jnp.int32, (z.hours, LANES), 1)
    low = lane < z.cols
    ga = Gather(z, own, full, ssem, rsem)

    barrier = pltpu.get_barrier_semaphore()
    for way in (UP, DOWN, RIGHT, LEFT, CORE):
        when_all(
            ga.has(way),
            lambda: pl.semaphore_signal(
                barrier, inc=1, device_id=ga.device(way), device_id_type=MESH
            ),
        )
    for s in range(1, z.parts):
        pl.semaphore_signal(
            barrier, inc=1, device_id=(me, (net + s) % z.parts), device_id_type=MESH
        )

    def mate(r):
        bit = 2**r
        return (me + bit - 2 * bit * ((me // bit) % 2), net)

    for r in range(z.rounds):
        pl.semaphore_signal(barrier, inc=1, device_id=mate(r), device_id_type=MESH)
    met = jnp.int32(z.parts + z.rounds)
    for way in (UP, DOWN, RIGHT, LEFT):
        for c in ga.has(way):
            met = met + c.astype(jnp.int32)

    loads = [
        pltpu.make_async_copy(h, v, msem.at[i])
        for i, (h, v) in enumerate(
            [
                (fac_h, fac), (line_h, line), (empty_h, empty), (full_h, dfull), (head_h, head),
                (avail_h, avail), (gen_h, gen), (chg_h, chg), (dis_h, dis), (base_h, base),
            ]
        )
    ]
    for c in loads:
        c.start()

    def own_copy(q):
        return pltpu.make_async_copy(own.at[q], full.at[q, me], msem.at[len(loads) + q])

    def lay_out(q):
        even = q % 2 == 0
        tile = pl.ds(pl.multiple_of((q // 2) * LANES, LANES), LANES)
        here = lax.broadcasted_iota(jnp.int32, (z.lines_local, LANES), 1) < z.cols
        for g in range(z.groups):
            for p in range(z.pairs):
                x = fac[g, 2 * p, :, tile]
                y = fac[g, 2 * p + 1, :, tile] if 2 * p + 1 < z.slots else jnp.zeros_like(x)
                keep = jnp.where(even, x, y)
                turn = pltpu.roll(jnp.where(even, y, x), z.cols, 1)
                own[q, g * z.lines_local : (g + 1) * z.lines_local, p * LANES : (p + 1) * LANES] = (
                    jnp.where(here == even, keep, turn)
                )

    def begin(q):
        lay_out(q)
        ga.start_own(q)
        own_copy(q).start()

    def sum_copy(r):
        return pltpu.make_async_remote_copy(
            src_ref=sums.at[r],
            dst_ref=sums_in.at[r],
            send_sem=tsem.at[r],
            recv_sem=tsem.at[z.rounds + r],
            device_id=mate(r),
            device_id_type=MESH,
        )

    loads[0].wait()
    lay_out(0)
    pl.semaphore_wait(barrier, met)
    ga.start_own(0)
    own_copy(0).start()

    for c in loads[1:4]:
        c.wait()

    def take_line(g, carry):
        cols = pl.ds(pl.multiple_of(g * z.lines, z.lines), z.lines)
        duals[g] = stacked(line[:, cols])
        parts_r[g * (z.pairs + 1) + z.pairs] = jnp.zeros((z.hours, LANES), f32)
        return carry

    lax.fori_loop(0, z.groups, take_line, 0)

    def find(m, carry):
        def in_group(g, carry):
            for k in range(2):
                found = jnp.int32(z.pairs)
                for p in range(z.pairs):
                    j = 2 * p + k
                    if j < z.slots:
                        block = lax.rem(pat[g, j] - net * z.groups + z.blocks, z.blocks)
                        found = jnp.where(block == m, p, found)
                tab[(k * z.blocks + m) * z.groups + g] = g * (z.pairs + 1) + found
            return carry

        return lax.fori_loop(0, z.groups, in_group, carry)

    lax.fori_loop(0, z.blocks, find, 0)

    at = (node[...] - net * z.nodes).astype(f32)
    block = jnp.floor((at + 0.5) / z.width)
    col = at - block * z.width
    unit = lax.broadcasted_iota(jnp.int32, at.shape, 1).astype(f32)
    pair_of = jnp.floor((unit + 0.5) / LANES)
    part_of = jnp.floor((col + 0.5) / z.cols)
    spot = (block - pair_of * z.per) * z.cols + col - part_of * z.cols
    for q in range(z.chunks):
        place[q] = jnp.where(part_of == q, spot, -1.0)

    back[...] = decayed_sums(empty[...] + dfull[...], 1.0 - loss[...], True)
    price[...] = jnp.zeros_like(price)
    out_line[...] = jnp.zeros_like(out_line)
    total[...] = jnp.zeros_like(total)
    for c in loads[4:]:
        c.wait()
    sums[0, :, : z.nodes] = jnp.sum(avail[...] * head[...], axis=0, keepdims=True)
    sums[0, :, z.nodes :] = jnp.sum(dfull[...], axis=0, keepdims=True)
    sum_copy(0).start()

    hour_r = lax.broadcasted_iota(jnp.int32, (z.hours, z.hours), 0)
    hour_c = lax.broadcasted_iota(jnp.int32, (z.hours, z.hours), 1)
    eye = hour_r == hour_c
    balance_col = jnp.sum(jnp.where(eye, balance[...], 0.0), axis=1, keepdims=True)

    def factor_copy(q, g):
        return pltpu.make_async_copy(
            full.at[q, :, pl.ds(pl.multiple_of(g * z.lines_local, 8), z.lines_local)],
            fbuf.at[g % 2], fsem.at[g % 2],
        )

    def image(q):
        factor_copy(q, 0).start()

        def group(g, carry):
            factor_copy(q, g).wait()

            @pl.when(g + 1 < z.groups)
            def _():
                factor_copy(q, g + 1).start()

            for c0 in range(0, z.wide, 2 * LANES):
                c1 = min(c0 + 2 * LANES, z.wide)
                w = fbuf[g % 2, :, :, c0:c1].reshape(z.lines, c1 - c0)
                hi, lo = split(w)
                wh[g, :, c0:c1] = hi
                wl[g, :, c0:c1] = lo
                r = dot(duals[g], hi)
                r = r[: z.hours] + r[z.hours :] + dot(duals[g, : z.hours], lo)
                for p in range(c0 // LANES, c1 // LANES):
                    parts_r[g * (z.pairs + 1) + p] = r[:, p * LANES - c0 : (p + 1) * LANES - c0]
            return carry

        lax.fori_loop(0, z.groups, group, 0)

    def collect(first, last):
        def pair(m, carry):
            found = []
            for k in range(2):
                for i in range(2):
                    x = jnp.zeros((z.hours, LANES), f32)
                    for g in range(z.groups):
                        x = x + parts_r[tab[(k * z.blocks + m * 2 + i) * z.groups + g]]
                    found.append(x)
            low0, low1, high0, high1 = found
            crossed = jnp.where(low, low1, high0)
            img[m] = jnp.where(low, low0, high1) + pltpu.roll(crossed, z.cols, 1)
            return carry

        lax.fori_loop(first, last, pair, 0)

    def img_copy(s):
        return pltpu.make_async_remote_copy(
            src_ref=img.at[pl.ds(s * half, half)],
            dst_ref=img_in.at[pl.ds((s - 1) * half, half)],
            send_sem=xsem.at[s - 1],
            recv_sem=xsem.at[z.parts - 1 + s - 1],
            device_id=(me, (net + s) % z.parts),
            device_id_type=MESH,
        )

    def inj_copy(s):
        return pltpu.make_async_remote_copy(
            src_ref=inj,
            dst_ref=inj_in.at[pl.ds((s - 1) * half, half)],
            send_sem=xsem.at[2 * (z.parts - 1) + s - 1],
            recv_sem=xsem.at[3 * (z.parts - 1) + s - 1],
            device_id=(me, (net - s + z.parts) % z.parts),
            device_id_type=MESH,
        )

    def hold(m, x):
        turned = pltpu.roll(x, z.cols, 1)
        zero = jnp.zeros_like(x)
        held[0, 2 * m] = stacked(jnp.where(low, x, zero))
        held[1, 2 * m] = stacked(jnp.where(low, zero, turned))
        held[0, 2 * m + 1] = stacked(jnp.where(low, turned, zero))
        held[1, 2 * m + 1] = stacked(jnp.where(low, zero, x))

    def dispatch(q):
        even = q % 2 == 0
        tile = (q // 2) * LANES

        def packed(ref, t):
            x = ref[:, pl.ds(pl.multiple_of((2 * t) * z.width + tile, LANES), LANES)]
            y = ref[:, pl.ds(pl.multiple_of((2 * t + 1) * z.width + tile, LANES), LANES)]
            here = lax.broadcasted_iota(jnp.int32, x.shape, 1) < z.cols
            keep = jnp.where(even, x, y)
            turn = pltpu.roll(jnp.where(even, y, x), z.cols, 1)
            return jnp.where(here == even, keep, turn)

        def pair(t, carry):
            image_t = img[t]
            for s in range(1, z.parts):
                image_t = image_t + img_in[(s - 1) * half + t]
            price_t = balance_col + image_t
            gen_t = packed(gen, t)
            moved = jnp.maximum(
                gen_t - primal_step * (packed(fuel, t) + price_t + packed(head, t)), 0.0
            )
            turned = pltpu.roll(moved, z.cols, 1)
            for i in range(2):
                cols = pl.ds(pl.multiple_of((2 * t + i) * z.width + tile, LANES), LANES)
                mine = jnp.where(even, moved if i == 0 else turned, turned if i == 0 else moved)
                gen_out[:, cols] = jnp.where(low == even, mine, gen_out[:, cols])
            units = pl.ds(pl.multiple_of(t * LANES, LANES), LANES)
            row = lax.broadcasted_iota(jnp.int32, (LANES, LANES), 0).astype(f32)
            marks = jnp.where(row == place[q, :, units], 1.0, 0.0).astype(bf16)
            hi, lo = split(price_t)
            cost = price[:, units] + (dot(hi, marks) + dot(lo, marks))
            price[:, units] = cost
            b = back[:, units]
            cap = power[:, units]
            c, d = chg[:, units], dis[:, units]
            next_c = jnp.minimum(jnp.maximum(c - store_step * (efficiency * b - cost), 0.0), cap)
            next_d = jnp.minimum(jnp.maximum(d - store_step * (cost - b / efficiency), 0.0), cap)
            out_c[:, units] = next_c
            out_d[:, units] = next_d
            hi, lo = split((2.0 * next_d - d) - (2.0 * next_c - c))
            inj[t] = (2.0 * moved - gen_t) + (dot_t(hi, marks) + dot_t(lo, marks))
            return carry

        lax.fori_loop(0, half, pair, 0)

    def hold_own(t, carry):
        x = inj[t]
        total[...] += x
        hold(t, x)
        return carry

    def hold_in(t, carry):
        x = inj_in[t]
        total[...] += x
        hold(half + t, x)
        return carry

    def flow(g, carry):
        cols = pl.ds(pl.multiple_of(g * z.lines, z.lines), z.lines)
        both = []
        for p in range(z.pairs):
            x = None
            for k in range(2):
                if 2 * p + k < z.slots:
                    m = lax.rem(pat[g, 2 * p + k] - net * z.groups + z.blocks, z.blocks)
                    y = held[k, m]
                    x = y if x is None else x + y
            both.append(x)
        both = jnp.concatenate(both, axis=1)
        r = dot_t(both, wh[g])
        r = r[: z.hours] + r[z.hours :] + dot_t(both[: z.hours], wl[g])
        out_line[:, cols] = out_line[:, cols] + r
        return carry

    steps = z.a
    lag = 2
    ready = -(-(steps + 2) // lag)

    def events(k, keep):
        found = []
        for o in range(lag):
            for t in range(steps, -1, -1):
                if (t - o) % lag == 0 and keep(t):
                    found.append((o, t, k - (t - o) // lag))
        last = steps + 1
        if keep(last):
            found.append((last % lag, last, k - last // lag))
        for _, t, q in found:
            live = jnp.logical_and(q >= 0, q < z.chunks)

            def act(t=t, q=q):
                if t == 0:
                    pl.when(q > 0)(lambda: begin(q))
                elif t <= steps:
                    ga.step(q, t - 1)
                else:
                    ga.finish(q)
                    own_copy(q).wait()

            pl.when(live)(act)

    def beat(k, carry):
        q = k - ready
        live = jnp.logical_and(q >= 0, q < z.chunks)

        for r in range(1, z.rounds + 1):
            @pl.when(k == r)
            def _():
                sum_copy(r - 1).wait_recv()
                sums[r] = sums[r - 1] + sums_in[r - 1]
                if r < z.rounds:
                    sum_copy(r).start()

        events(k, lambda t: t == 0)

        @pl.when(live)
        def _():
            image(q)

            @pl.when(q > 0)
            def _():
                for s in range(1, z.parts):
                    img_copy(s).wait_send()
                    inj_copy(s).wait_send()

            for s in range(1, z.parts):
                collect(s * half, (s + 1) * half)
                img_copy(s).start()
            collect(0, half)

        events(k, lambda t: 0 < t < steps and t % lag == 0)

        @pl.when(live)
        def _():
            for s in range(1, z.parts):
                img_copy(s).wait_recv()
            dispatch(q)
            for s in range(1, z.parts):
                inj_copy(s).start()
            lax.fori_loop(0, half, hold_own, 0)
            for s in range(1, z.parts):
                inj_copy(s).wait_recv()
            lax.fori_loop(0, half * (z.parts - 1), hold_in, 0)
            lax.fori_loop(0, z.groups, flow, 0)

        events(k, lambda t: t >= steps or t % lag)
        return carry

    lax.fori_loop(0, z.chunks + ready, beat, 0)

    for s in range(1, z.parts):
        img_copy(s).wait_send()
        inj_copy(s).wait_send()

    for g in range(z.groups):
        cols = slice(g * z.lines, (g + 1) * z.lines)
        moved = line[:, cols] + dual_step * out_line[:, cols]
        floor = -limit[:, cols] - base[:, cols]
        ceiling = limit[:, cols] - base[:, cols]
        out_line[:, cols] = moved - dual_step * jnp.minimum(
            jnp.maximum(moved / dual_step, floor), ceiling
        )
    found = sums[z.rounds]
    next_plant = jnp.maximum(
        plant[...] - primal_step * (plant_cost[...] - found[:, : z.nodes] / (z.scen * z.hours)), 0.0
    )
    next_store = jnp.maximum(
        stored[...] - primal_step * (store_cost[...] - found[:, z.nodes :] / (z.scen * z.hours)), 0.0
    )
    out_p[...] = next_plant
    out_s[...] = next_store
    extra_plant = 2.0 * next_plant - plant[...]
    extra_store = 2.0 * next_store - stored[...]
    out_h[...] = jnp.maximum(
        head[...] + dual_step * ((2.0 * gen_out[...] - gen[...]) - avail[...] * extra_plant), 0.0
    )
    extra_c = 2.0 * out_c[...] - chg[...]
    extra_d = 2.0 * out_d[...] - dis[...]
    levels = decayed_sums(efficiency * extra_c - extra_d / efficiency, 1.0 - loss[...], False)
    out_e[...] = jnp.minimum(empty[...] + level_step * levels, 0.0)
    out_f[...] = jnp.maximum(dfull[...] + level_step * (levels - extra_store), 0.0)
    col_total = jnp.sum(total[...], axis=1, keepdims=True)
    row_total = jnp.sum(jnp.where(eye, col_total, 0.0), axis=0, keepdims=True)
    out_b[...] = balance[...] + dual_step * (row_total / (z.blocks * z.width) - demand[...])

    for r in range(z.rounds):
        sum_copy(r).wait_send()

    def drained(q, carry):
        ga.drain(q)
        return carry

    lax.fori_loop(0, z.chunks, drained, 0)


def run_step(z, pat, big, small):
    h, n, st, ln = z.hours, z.nodes, z.stores, z.groups * z.lines
    half = z.groups // z.per
    others = z.parts - 1
    hbm = pl.BlockSpec(memory_space=pltpu.HBM)
    vmem = pl.BlockSpec(memory_space=pltpu.VMEM)
    smem = pl.BlockSpec(memory_space=pltpu.SMEM)

    def shape(*dims):
        return jax.ShapeDtypeStruct(dims, f32)

    def buffer(*dims, dtype=f32):
        return pltpu.VMEM(dims, dtype)

    outs = [
        shape(z.chunks, z.scen, z.rows, z.wide), shape(h, n), shape(h, st), shape(h, st),
        shape(1, n), shape(1, st), shape(1, h), shape(h, ln), shape(h, n), shape(h, st), shape(h, st),
    ]
    return pl.pallas_call(
        functools.partial(step_kernel, z),
        out_shape=outs,
        in_specs=[smem] + [hbm] * len(big) + [vmem] * len(small),
        out_specs=[hbm] + [vmem] * (len(outs) - 1),
        scratch_shapes=[
            buffer(z.groups, 2 * h, z.lines, dtype=bf16),
            buffer(z.groups, z.lines, z.wide, dtype=bf16),
            buffer(z.groups, z.lines, z.wide, dtype=bf16),
            buffer(2, z.scen, z.lines_local, z.wide),
            buffer(z.groups, z.slots, z.lines_local, z.width),
            buffer(z.chunks, z.rows, z.wide),
            buffer(z.groups * (z.pairs + 1), h, LANES),
            buffer(z.parts * half, h, LANES),
            buffer(others * half, h, LANES),
            buffer(half, h, LANES),
            buffer(others * half, h, LANES),
            buffer(2, z.blocks, 2 * h, LANES, dtype=bf16),
            buffer(h, ln),
            buffer(h, ln),
        ]
        + [buffer(h, n)] * 3
        + [buffer(h, st)] * 6
        + [
            buffer(z.chunks, 1, st),
            buffer(h, LANES),
            buffer(z.rounds + 1, 1, n + st),
            buffer(z.rounds, 1, n + st),
            pltpu.SMEM((2 * z.blocks * z.groups,), jnp.int32),
            pltpu.SemaphoreType.DMA((z.chunks * 2 * (z.scen // 2) * 5,)),
            pltpu.SemaphoreType.DMA((z.chunks * 2 * z.scen,)),
            pltpu.SemaphoreType.DMA((2,)),
            pltpu.SemaphoreType.DMA((4 * others,)),
            pltpu.SemaphoreType.DMA((len(big) + z.chunks,)),
            pltpu.SemaphoreType.DMA((2 * z.rounds,)),
        ],
        compiler_params=pltpu.CompilerParams(
            vmem_limit_bytes=VMEM_BYTES, collective_id=0, has_side_effects=True
        ),
        cost_estimate=pl.CostEstimate(
            flops=12 * h * z.groups * z.lines * z.slots * z.width,
            bytes_accessed=12 * z.groups * z.lines * z.slots * z.width,
            transcendentals=0,
        ),
        name="iteration",
    )(pat, *big, *small)


def body(
    generation, charging, discharging, plant_capacity, store_capacity, dual_balance, dual_line,
    dual_headroom, dual_empty, dual_full, availability, demand, line_base, line_limit, fuel_cost,
    plant_cost, store_cost, self_loss, power_limit, store_node, line_factors, block_pattern,
):
    z = Sizes(lax.axis_size("scen"), lax.axis_size("net"), generation, line_factors, store_node)
    big = [
        line_factors.transpose(0, 2, 1, 3), dual_line[0], line_base[0], generation[0],
        dual_headroom[0], availability[0], charging[0], discharging[0], dual_empty[0], dual_full[0],
    ]
    small = [dual_balance, demand] + [
        x[None]
        for x in (
            fuel_cost, self_loss, power_limit, store_node, line_limit,
            plant_capacity, plant_cost, store_capacity, store_cost,
        )
    ]
    outs = run_step(z, block_pattern, big, small)
    gen, chg, dis, plant, stored, balance, line, head, empty, full = outs[1:]
    return (
        gen[None], chg[None], dis[None], plant[0], stored[0], balance,
        line[None], head[None], empty[None], full[None],
    )


def solution(mesh):
    row = P("scen", None, "net")
    placed = (
        row, row, row, P("net"), P("net"), P("scen", None), row, row, row, row, row,
        P("scen", None), row, P("net"), P("net"), P("net"), P("net"), P("net"), P("net"), P("net"),
        P("net", "scen", None, None), P("net", None),
    )
    return jax.shard_map(
        body,
        mesh=mesh,
        in_specs=placed,
        out_specs=(row, row, row, P("net"), P("net"), P("scen", None), row, row, row, row),
        check_vma=False,
    )
```

time: 319 us -> 326 us (1.022)
  Pallas kernels: 78.4 us -> 313 us
  waiting for transfers between devices: 136 us -> 0 us
  blocking collectives: 64.6 us -> 0 us
  between operations: 14.2 us -> 0.7 us
  other arithmetic: 8.78 us -> 0 us
  starting transfers between devices: 5.67 us -> 0 us
    pallas_call x8 -> x1, Pallas kernels: 78.4 us -> 313 us  [run_step(): pl.pallas_call(functools.partial(step_kernel, z), out_shape=outs, in_spec...]
    all_gather x2 -> x0, waiting for transfers between devices: 80.4 us -> none  [body(): gathered.append(lax.all_gather(piece, 'scen', axis=0))]
    psum x1 -> x0, blocking collectives: 64.6 us -> none  [body(): totals = lax.psum(jnp.concatenate([plant_part, store_part]), 'scen')]
    ppermute x4 -> x0, waiting for transfers between devices: 55.2 us -> none  [the longest x2 30.3 us: body(): lax.ppermute(partial_images[s], 'net', [(i, (i + s) % parts) for i in ran...]
    unnamed x36 -> x28, local copies, waits for them, and re-layouts: 2.78 us -> 10.9 us
    ppermute x4 -> x0, starting transfers between devices: 5.59 us -> none  [the longest x2 2.87 us: body(): lax.ppermute(inj, 'net', [(i, (i - s) % parts) for i in range(parts)])]
    slice x3 -> x0, local copies, waits for them, and re-layouts: 3.59 us -> none  [body(): piece = line_factors[:, :, :, q * LANES:(q + 1) * LANES]]
    another operation x3 -> x0, local copies, waits for them, and re-layouts: 3.34 us -> none  [the longest x2 2.58 us: body(): gathered.append(lax.all_gather(piece, 'scen', axis=0))]
  transfers between devices with their start and end apart: 6 -> 0, of which waited for: 6 -> 0; matrix products, arithmetic and copies ran while one was open for 3% -> 0% of each run, Pallas kernels for 13% -> 0%
where the time goes in v1:
time: 326 us; the launch traced here: 325 us
  Pallas kernels  313 us (96%)
  local copies, waits for them, and re-layouts  10.9 us (3%)
    pallas_call x1, Pallas kernels, run_step(): pl.pallas_call(functools.partial(step_kernel, z), out_shape=outs, in_spec...  313 us
    unnamed x28, local copies, waits for them, and re-layouts  10.9 us

profile of v1, /device:TPU:0, one launch (start us, length us, event | category | flops | bytes accessed | tf_op | source)
XLA Modules:
  0.0 324.6 jit_solution(10713479655527826656)
XLA Ops:
  0.7 313.0 %iteration.1 = (f32[4,16,256,640]{3,2,1,0:T(8,128)}, f32[168,2048]{1,0:T(8,128)}, f32[168,512]{1,0:T(8,128)}, f32[168,512]{1,0:T(8,128)}, f32[1,2048]{1,0:T(1,12...) custom-call(s32[8,10]{1,0:T(8,128)} %pat.1, ...), custom_call_target="tpu_custom_call" | custom-call | flops 21139292160 | bytes 125829120 | tf_op jit(solution)/shard_map/iteration/pallas_call | solution.py:637
  313.6 0.0 copy-start.5
  313.6 0.0 copy-start.4
  313.6 0.0 copy-start.6
  313.7 0.0 copy-start
  313.7 2.7 copy.42
  316.4 0.0 copy-done.5
  316.4 0.0 copy-start.7
  316.4 0.0 copy-start.8
  316.4 0.7 copy.43
  317.1 0.0 copy-done.4
  317.1 0.7 copy.44
  317.8 0.0 copy-done.6
  317.8 0.6 copy.45
  318.4 0.0 copy-done.7
  318.4 0.6 copy.46
  319.0 0.0 copy-done.8
  319.0 0.6 copy.47
  319.6 0.0 copy-done
  319.6 0.0 copy-start.1
  319.6 1.5 copy.48
  321.1 0.8 copy-done.1
  321.9 0.0 copy-start.3
  321.9 0.0 copy-start.2
  321.9 1.1 copy.49
  323.0 0.1 copy-done.3
  323.1 0.7 copy.50
  323.8 0.0 copy-done.2
  323.9 0.7 copy.51
Async XLA Ops:
  313.6 2.7 copy-start.5
  313.6 3.5 %copy-start.4 = (f32[168,512]{1,0:T(8,128)S(1)}, f32[168,512]{1,0:T(8,128)}, u32[]{:S(2)}) copy-start(f32[168,512]{1,0:T(8,128)} %get-tuple-element.22) | copy-start | bytes 1032196
  313.6 4.2 %copy-start.6 = (f32[1,2048]{1,0:T(1,128)S(1)}, f32[1,2048]{1,0:T(1,128)}, u32[]{:S(2)}) copy-start(f32[1,2048]{1,0:T(1,128)} %get-tuple-element.23) | copy-start | bytes 24580
  313.7 5.9 %copy-start = (f32[168,4096]{1,0:T(8,128)S(1)}, f32[168,4096]{1,0:T(8,128)}, u32[]{:S(2)}) copy-start(f32[168,4096]{1,0:T(8,128)} %get-tuple-element.26) | copy-start | bytes 8257540
  316.4 2.1 copy-start.7
  316.4 2.7 copy-start.8
  319.6 2.3 copy-start.1
  321.9 1.2 copy-start.3
  321.9 1.9 copy-start.2

commit v2 on v1

--- a/solution.py
+++ b/solution.py
@@ -210,10 +210,11 @@
 def step_kernel(
     z, pat, fac_h, line_h, base_h, gen_h, head_h, avail_h, chg_h, dis_h, empty_h, full_h,
     balance, demand, fuel, loss, power, node, limit, plant, plant_cost, stored, store_cost,
-    full, gen_out, out_c, out_d, out_p, out_s, out_b, out_line, out_h, out_e, out_f,
+    full, out_gen, out_c, out_d, out_p, out_s, out_line, out_h, out_e, out_f, out_b,
     duals, wh, wl, fbuf, fac, own, parts_r, img, img_in, inj, inj_in, held,
-    line, base, gen, head, avail, chg, dis, empty, dfull, back, price, place, total, sums, sums_in, tab,
-    ssem, rsem, fsem, xsem, msem, tsem,
+    line, base, gen, head, avail, chg, dis, empty, dfull, back, price, next_c, next_d, next_e, next_f,
+    place, total, sums, sums_in, acc, next_gen, next_h, next_p, next_s, level, tab,
+    ssem, rsem, fsem, xsem, msem, tsem, osem,
 ):
     me, net = lax.axis_index("scen"), lax.axis_index("net")
     half = z.groups // z.per
@@ -295,16 +296,15 @@
     ga.start_own(0)
     own_copy(0).start()
 
-    for c in loads[1:4]:
-        c.wait()
+    hour_r = lax.broadcasted_iota(jnp.int32, (z.hours, z.hours), 0)
+    hour_c = lax.broadcasted_iota(jnp.int32, (z.hours, z.hours), 1)
+    eye = hour_r == hour_c
 
     def take_line(g, carry):
         cols = pl.ds(pl.multiple_of(g * z.lines, z.lines), z.lines)
         duals[g] = stacked(line[:, cols])
         parts_r[g * (z.pairs + 1) + z.pairs] = jnp.zeros((z.hours, LANES), f32)
         return carry
-
-    lax.fori_loop(0, z.groups, take_line, 0)
 
     def find(m, carry):
         def in_group(g, carry):
@@ -320,32 +320,31 @@
 
         return lax.fori_loop(0, z.groups, in_group, carry)
 
-    lax.fori_loop(0, z.blocks, find, 0)
-
-    at = (node[...] - net * z.nodes).astype(f32)
-    block = jnp.floor((at + 0.5) / z.width)
-    col = at - block * z.width
-    unit = lax.broadcasted_iota(jnp.int32, at.shape, 1).astype(f32)
-    pair_of = jnp.floor((unit + 0.5) / LANES)
-    part_of = jnp.floor((col + 0.5) / z.cols)
-    spot = (block - pair_of * z.per) * z.cols + col - part_of * z.cols
-    for q in range(z.chunks):
-        place[q] = jnp.where(part_of == q, spot, -1.0)
-
-    back[...] = decayed_sums(empty[...] + dfull[...], 1.0 - loss[...], True)
-    price[...] = jnp.zeros_like(price)
-    out_line[...] = jnp.zeros_like(out_line)
-    total[...] = jnp.zeros_like(total)
-    for c in loads[4:]:
-        c.wait()
-    sums[0, :, : z.nodes] = jnp.sum(avail[...] * head[...], axis=0, keepdims=True)
-    sums[0, :, z.nodes :] = jnp.sum(dfull[...], axis=0, keepdims=True)
-    sum_copy(0).start()
-
-    hour_r = lax.broadcasted_iota(jnp.int32, (z.hours, z.hours), 0)
-    hour_c = lax.broadcasted_iota(jnp.int32, (z.hours, z.hours), 1)
-    eye = hour_r == hour_c
-    balance_col = jnp.sum(jnp.where(eye, balance[...], 0.0), axis=1, keepdims=True)
+    def prepare_sums():
+        for c in loads[1:]:
+            c.wait()
+        sums[0, :, : z.nodes] = jnp.sum(avail[...] * head[...], axis=0, keepdims=True)
+        sums[0, :, z.nodes :] = jnp.sum(dfull[...], axis=0, keepdims=True)
+        sum_copy(0).start()
+        price[...] = jnp.zeros_like(price)
+        total[...] = jnp.zeros_like(total)
+        acc[...] = jnp.zeros_like(acc)
+        lax.fori_loop(0, z.groups, take_line, 0)
+
+    def prepare_tables():
+        lax.fori_loop(0, z.blocks, find, 0)
+        at = (node[...] - net * z.nodes).astype(f32)
+        block = jnp.floor((at + 0.5) / z.width)
+        col = at - block * z.width
+        unit = lax.broadcasted_iota(jnp.int32, at.shape, 1).astype(f32)
+        pair_of = jnp.floor((unit + 0.5) / LANES)
+        part_of = jnp.floor((col + 0.5) / z.cols)
+        spot = (block - pair_of * z.per) * z.cols + col - part_of * z.cols
+        for q in range(z.chunks):
+            place[q] = jnp.where(part_of == q, spot, -1.0)
+        back[...] = decayed_sums(empty[...] + dfull[...], 1.0 - loss[...], True)
+        column = jnp.sum(jnp.where(eye, balance[...], 0.0), axis=1, keepdims=True)
+        level[...] = jnp.broadcast_to(column, level.shape)
 
     def factor_copy(q, g):
         return pltpu.make_async_copy(
@@ -377,41 +376,52 @@
 
         lax.fori_loop(0, z.groups, group, 0)
 
-    def collect(first, last):
-        def pair(m, carry):
-            found = []
-            for k in range(2):
-                for i in range(2):
-                    x = jnp.zeros((z.hours, LANES), f32)
-                    for g in range(z.groups):
-                        x = x + parts_r[tab[(k * z.blocks + m * 2 + i) * z.groups + g]]
-                    found.append(x)
-            low0, low1, high0, high1 = found
-            crossed = jnp.where(low, low1, high0)
-            img[m] = jnp.where(low, low0, high1) + pltpu.roll(crossed, z.cols, 1)
-            return carry
-
-        lax.fori_loop(first, last, pair, 0)
-
-    def img_copy(s):
+    def collect(m):
+        found = []
+        for k in range(2):
+            for i in range(2):
+                x = jnp.zeros((z.hours, LANES), f32)
+                for g in range(z.groups):
+                    x = x + parts_r[tab[(k * z.blocks + m * 2 + i) * z.groups + g]]
+                found.append(x)
+        low0, low1, high0, high1 = found
+        crossed = jnp.where(low, low1, high0)
+        img[m] = jnp.where(low, low0, high1) + pltpu.roll(crossed, z.cols, 1)
+
+    others = z.parts - 1
+
+    def img_copy(s, t):
+        i = (s - 1) * half + t
         return pltpu.make_async_remote_copy(
-            src_ref=img.at[pl.ds(s * half, half)],
-            dst_ref=img_in.at[pl.ds((s - 1) * half, half)],
-            send_sem=xsem.at[s - 1],
-            recv_sem=xsem.at[z.parts - 1 + s - 1],
+            src_ref=img.at[s * half + t],
+            dst_ref=img_in.at[i],
+            send_sem=xsem.at[i],
+            recv_sem=xsem.at[others * half + i],
             device_id=(me, (net + s) % z.parts),
             device_id_type=MESH,
         )
 
-    def inj_copy(s):
+    def inj_copy(s, t):
+        i = (s - 1) * half + t
         return pltpu.make_async_remote_copy(
-            src_ref=inj,
-            dst_ref=inj_in.at[pl.ds((s - 1) * half, half)],
-            send_sem=xsem.at[2 * (z.parts - 1) + s - 1],
-            recv_sem=xsem.at[3 * (z.parts - 1) + s - 1],
+            src_ref=inj.at[t],
+            dst_ref=inj_in.at[i],
+            send_sem=xsem.at[2 * others * half + i],
+            recv_sem=xsem.at[3 * others * half + i],
             device_id=(me, (net - s + z.parts) % z.parts),
             device_id_type=MESH,
         )
+
+    def each(fn):
+        def one(i, carry):
+            fn(i // half + 1, i % half)
+            return carry
+
+        lax.fori_loop(0, others * half, one, 0)
+
+    def all_sent():
+        each(lambda s, t: img_copy(s, t).wait_send())
+        each(lambda s, t: inj_copy(s, t).wait_send())
 
     def hold(m, x):
         turned = pltpu.roll(x, z.cols, 1)
@@ -436,8 +446,9 @@
         def pair(t, carry):
             image_t = img[t]
             for s in range(1, z.parts):
+                img_copy(s, t).wait_recv()
                 image_t = image_t + img_in[(s - 1) * half + t]
-            price_t = balance_col + image_t
+            price_t = level[...] + image_t
             gen_t = packed(gen, t)
             moved = jnp.maximum(
                 gen_t - primal_step * (packed(fuel, t) + price_t + packed(head, t)), 0.0
@@ -446,7 +457,7 @@
             for i in range(2):
                 cols = pl.ds(pl.multiple_of((2 * t + i) * z.width + tile, LANES), LANES)
                 mine = jnp.where(even, moved if i == 0 else turned, turned if i == 0 else moved)
-                gen_out[:, cols] = jnp.where(low == even, mine, gen_out[:, cols])
+                next_gen[:, cols] = jnp.where(low == even, mine, next_gen[:, cols])
             units = pl.ds(pl.multiple_of(t * LANES, LANES), LANES)
             row = lax.broadcasted_iota(jnp.int32, (LANES, LANES), 0).astype(f32)
             marks = jnp.where(row == place[q, :, units], 1.0, 0.0).astype(bf16)
@@ -456,12 +467,14 @@
             b = back[:, units]
             cap = power[:, units]
             c, d = chg[:, units], dis[:, units]
-            next_c = jnp.minimum(jnp.maximum(c - store_step * (efficiency * b - cost), 0.0), cap)
-            next_d = jnp.minimum(jnp.maximum(d - store_step * (cost - b / efficiency), 0.0), cap)
-            out_c[:, units] = next_c
-            out_d[:, units] = next_d
-            hi, lo = split((2.0 * next_d - d) - (2.0 * next_c - c))
+            new_c = jnp.minimum(jnp.maximum(c - store_step * (efficiency * b - cost), 0.0), cap)
+            new_d = jnp.minimum(jnp.maximum(d - store_step * (cost - b / efficiency), 0.0), cap)
+            next_c[:, units] = new_c
+            next_d[:, units] = new_d
+            hi, lo = split((2.0 * new_d - d) - (2.0 * new_c - c))
             inj[t] = (2.0 * moved - gen_t) + (dot_t(hi, marks) + dot_t(lo, marks))
+            for s in range(1, z.parts):
+                inj_copy(s, t).start()
             return carry
 
         lax.fori_loop(0, half, pair, 0)
@@ -472,13 +485,13 @@
         hold(t, x)
         return carry
 
-    def hold_in(t, carry):
-        x = inj_in[t]
+    def hold_in(s, t):
+        inj_copy(s, t).wait_recv()
+        x = inj_in[(s - 1) * half + t]
         total[...] += x
-        hold(half + t, x)
-        return carry
-
-    def flow(g, carry):
+        hold(s * half + t, x)
+
+    def flow(q, g):
         cols = pl.ds(pl.multiple_of(g * z.lines, z.lines), z.lines)
         both = []
         for p in range(z.pairs):
@@ -492,128 +505,156 @@
         both = jnp.concatenate(both, axis=1)
         r = dot_t(both, wh[g])
         r = r[: z.hours] + r[z.hours :] + dot_t(both[: z.hours], wl[g])
-        out_line[:, cols] = out_line[:, cols] + r
+        r = acc[:, cols] + r
+
+        @pl.when(q < z.chunks - 1)
+        def _():
+            acc[:, cols] = r
+
+        @pl.when(q == z.chunks - 1)
+        def _():
+            moved = line[:, cols] + dual_step * r
+            floor = -limit[:, cols] - base[:, cols]
+            ceiling = limit[:, cols] - base[:, cols]
+            acc[:, cols] = moved - dual_step * jnp.minimum(
+                jnp.maximum(moved / dual_step, floor), ceiling
+            )
+            line_out(g).start()
+
+
+    def line_out(g):
+        cols = pl.ds(pl.multiple_of(g * z.lines, z.lines), z.lines)
+        return pltpu.make_async_copy(acc.at[:, cols], out_line.at[:, cols], osem.at[g])
+
+    results = [
+        pltpu.make_async_copy(v, h, osem.at[z.groups + i])
+        for i, (v, h) in enumerate(
+            [
+                (next_gen, out_gen), (next_c, out_c), (next_d, out_d), (next_p, out_p),
+                (next_s, out_s), (next_h, out_h), (next_e, out_e), (next_f, out_f),
+            ]
+        )
+    ]
+
+    def settle():
+        for c in results[:3]:
+            c.start()
+        found = sums[z.rounds]
+        next_plant = jnp.maximum(
+            plant[...] - primal_step * (plant_cost[...] - found[:, : z.nodes] / (z.scen * z.hours)), 0.0
+        )
+        next_store = jnp.maximum(
+            stored[...] - primal_step * (store_cost[...] - found[:, z.nodes :] / (z.scen * z.hours)), 0.0
+        )
+        next_p[...] = next_plant
+        next_s[...] = next_store
+        extra_plant = 2.0 * next_plant - plant[...]
+        extra_store = 2.0 * next_store - stored[...]
+        next_h[...] = jnp.maximum(
+            head[...] + dual_step * ((2.0 * next_gen[...] - gen[...]) - avail[...] * extra_plant), 0.0
+        )
+        for c in results[3:6]:
+            c.start()
+        extra_c = 2.0 * next_c[...] - chg[...]
+        extra_d = 2.0 * next_d[...] - dis[...]
+        levels = decayed_sums(efficiency * extra_c - extra_d / efficiency, 1.0 - loss[...], False)
+        next_e[...] = jnp.minimum(empty[...] + level_step * levels, 0.0)
+        next_f[...] = jnp.maximum(dfull[...] + level_step * (levels - extra_store), 0.0)
+        for c in results[6:]:
+            c.start()
+
+    steps = z.a
+    points = 3
+
+    def event(k, t):
+        q = k - t // points
+
+        def act():
+            if t == 0:
+                pl.when(q > 0)(lambda: begin(q))
+            else:
+                ga.step(q, t - 1)
+            if t == steps:
+                ga.finish(q)
+                own_copy(q).wait()
+
+        pl.when(jnp.logical_and(q >= 0, q < z.chunks))(act)
+
+    ready = steps // points
+    turn = steps % points
+
+    def make_image(q):
+        pl.when(q > 0)(all_sent)
+        image(q)
+
+        def send(s, t):
+            collect(s * half + t)
+            img_copy(s, t).start()
+
+        each(send)
+        pl.loop(0, half)(collect)
+
+    def make_dispatch(q):
+        dispatch(q)
+        lax.fori_loop(0, half, hold_own, 0)
+        pl.when(q == z.chunks - 1)(settle)
+        ga.drain(q)
+
+    def make_flows(q):
+        each(hold_in)
+        pl.loop(0, z.groups)(functools.partial(flow, q))
+
+    tasks = [[] for _ in range(points)]
+    for i, task in enumerate((make_image, make_dispatch, make_flows)):
+        tasks[(turn + i) % points].append((ready + (turn + i) // points, task))
+
+    def beat(k, carry):
+        for o in range(points):
+            for r in range(1, z.rounds + 1):
+                if r % points == o:
+                    @pl.when(k == r // points)
+                    def _():
+                        sum_copy(r - 1).wait_recv()
+                        sums[r] = sums[r - 1] + sums_in[r - 1]
+                        if r < z.rounds:
+                            sum_copy(r).start()
+
+            for t in range(o, steps + 1, points):
+                event(k, t)
+            if o == 0:
+                pl.when(k == 0)(prepare_sums)
+            if o == 1:
+                pl.when(k == 0)(prepare_tables)
+            for late, task in tasks[o]:
+                q = k - late
+                pl.when(jnp.logical_and(q >= 0, q < z.chunks))(functools.partial(task, q))
         return carry
 
-    steps = z.a
-    lag = 2
-    ready = -(-(steps + 2) // lag)
-
-    def events(k, keep):
-        found = []
-        for o in range(lag):
-            for t in range(steps, -1, -1):
-                if (t - o) % lag == 0 and keep(t):
-                    found.append((o, t, k - (t - o) // lag))
-        last = steps + 1
-        if keep(last):
-            found.append((last % lag, last, k - last // lag))
-        for _, t, q in found:
-            live = jnp.logical_and(q >= 0, q < z.chunks)
-
-            def act(t=t, q=q):
-                if t == 0:
-                    pl.when(q > 0)(lambda: begin(q))
-                elif t <= steps:
-                    ga.step(q, t - 1)
-                else:
-                    ga.finish(q)
-                    own_copy(q).wait()
-
-            pl.when(live)(act)
-
-    def beat(k, carry):
-        q = k - ready
-        live = jnp.logical_and(q >= 0, q < z.chunks)
-
-        for r in range(1, z.rounds + 1):
-            @pl.when(k == r)
-            def _():
-                sum_copy(r - 1).wait_recv()
-                sums[r] = sums[r - 1] + sums_in[r - 1]
-                if r < z.rounds:
-                    sum_copy(r).start()
-
-        events(k, lambda t: t == 0)
-
-        @pl.when(live)
-        def _():
-            image(q)
-
-            @pl.when(q > 0)
-            def _():
-                for s in range(1, z.parts):
-                    img_copy(s).wait_send()
-                    inj_copy(s).wait_send()
-
-            for s in range(1, z.parts):
-                collect(s * half, (s + 1) * half)
-                img_copy(s).start()
-            collect(0, half)
-
-        events(k, lambda t: 0 < t < steps and t % lag == 0)
-
-        @pl.when(live)
-        def _():
-            for s in range(1, z.parts):
-                img_copy(s).wait_recv()
-            dispatch(q)
-            for s in range(1, z.parts):
-                inj_copy(s).start()
-            lax.fori_loop(0, half, hold_own, 0)
-            for s in range(1, z.parts):
-                inj_copy(s).wait_recv()
-            lax.fori_loop(0, half * (z.parts - 1), hold_in, 0)
-            lax.fori_loop(0, z.groups, flow, 0)
-
-        events(k, lambda t: t >= steps or t % lag)
-        return carry
-
-    lax.fori_loop(0, z.chunks + ready, beat, 0)
-
-    for s in range(1, z.parts):
-        img_copy(s).wait_send()
-        inj_copy(s).wait_send()
-
-    for g in range(z.groups):
-        cols = slice(g * z.lines, (g + 1) * z.lines)
-        moved = line[:, cols] + dual_step * out_line[:, cols]
-        floor = -limit[:, cols] - base[:, cols]
-        ceiling = limit[:, cols] - base[:, cols]
-        out_line[:, cols] = moved - dual_step * jnp.minimum(
-            jnp.maximum(moved / dual_step, floor), ceiling
-        )
-    found = sums[z.rounds]
-    next_plant = jnp.maximum(
-        plant[...] - primal_step * (plant_cost[...] - found[:, : z.nodes] / (z.scen * z.hours)), 0.0
-    )
-    next_store = jnp.maximum(
-        stored[...] - primal_step * (store_cost[...] - found[:, z.nodes :] / (z.scen * z.hours)), 0.0
-    )
-    out_p[...] = next_plant
-    out_s[...] = next_store
-    extra_plant = 2.0 * next_plant - plant[...]
-    extra_store = 2.0 * next_store - stored[...]
-    out_h[...] = jnp.maximum(
-        head[...] + dual_step * ((2.0 * gen_out[...] - gen[...]) - avail[...] * extra_plant), 0.0
-    )
-    extra_c = 2.0 * out_c[...] - chg[...]
-    extra_d = 2.0 * out_d[...] - dis[...]
-    levels = decayed_sums(efficiency * extra_c - extra_d / efficiency, 1.0 - loss[...], False)
-    out_e[...] = jnp.minimum(empty[...] + level_step * levels, 0.0)
-    out_f[...] = jnp.maximum(dfull[...] + level_step * (levels - extra_store), 0.0)
+    lax.fori_loop(0, z.chunks + ready + (turn + 2) // points, beat, 0)
+
     col_total = jnp.sum(total[...], axis=1, keepdims=True)
     row_total = jnp.sum(jnp.where(eye, col_total, 0.0), axis=0, keepdims=True)
     out_b[...] = balance[...] + dual_step * (row_total / (z.blocks * z.width) - demand[...])
-
+    all_sent()
     for r in range(z.rounds):
         sum_copy(r).wait_send()
-
-    def drained(q, carry):
-        ga.drain(q)
-        return carry
-
-    lax.fori_loop(0, z.chunks, drained, 0)
+    for c in results:
+        c.wait()
+    for g in range(z.groups):
+        line_out(g).wait()
+
+
+def hand_on(n, *refs):
+    held, into, out = refs[2 * n : 3 * n], refs[3 * n], refs[3 * n + 1]
+    loads = [pltpu.make_async_copy(refs[i], held[i], into.at[i]) for i in range(n)]
+    stores = [pltpu.make_async_copy(held[i], refs[n + i], out.at[i]) for i in range(n)]
+    for c in loads:
+        c.start()
+    for a, b in zip(loads, stores):
+        a.wait()
+        b.start()
+    for c in stores:
+        c.wait()
 
 
 def run_step(z, pat, big, small):
@@ -632,13 +673,13 @@
 
     outs = [
         shape(z.chunks, z.scen, z.rows, z.wide), shape(h, n), shape(h, st), shape(h, st),
-        shape(1, n), shape(1, st), shape(1, h), shape(h, ln), shape(h, n), shape(h, st), shape(h, st),
+        shape(1, n), shape(1, st), shape(h, ln), shape(h, n), shape(h, st), shape(h, st), shape(1, h),
     ]
     return pl.pallas_call(
         functools.partial(step_kernel, z),
         out_shape=outs,
         in_specs=[smem] + [hbm] * len(big) + [vmem] * len(small),
-        out_specs=[hbm] + [vmem] * (len(outs) - 1),
+        out_specs=[hbm] * (len(outs) - 1) + [vmem],
         scratch_shapes=[
             buffer(z.groups, 2 * h, z.lines, dtype=bf16),
             buffer(z.groups, z.lines, z.wide, dtype=bf16),
@@ -656,19 +697,26 @@
             buffer(h, ln),
         ]
         + [buffer(h, n)] * 3
-        + [buffer(h, st)] * 6
+        + [buffer(h, st)] * 10
         + [
             buffer(z.chunks, 1, st),
             buffer(h, LANES),
             buffer(z.rounds + 1, 1, n + st),
             buffer(z.rounds, 1, n + st),
+            buffer(h, ln),
+            buffer(h, n),
+            buffer(h, n),
+            buffer(1, n),
+            buffer(1, st),
+            buffer(h, LANES),
             pltpu.SMEM((2 * z.blocks * z.groups,), jnp.int32),
             pltpu.SemaphoreType.DMA((z.chunks * 2 * (z.scen // 2) * 5,)),
             pltpu.SemaphoreType.DMA((z.chunks * 2 * z.scen,)),
             pltpu.SemaphoreType.DMA((2,)),
-            pltpu.SemaphoreType.DMA((4 * others,)),
+            pltpu.SemaphoreType.DMA((4 * others * half,)),
             pltpu.SemaphoreType.DMA((len(big) + z.chunks,)),
             pltpu.SemaphoreType.DMA((2 * z.rounds,)),
+            pltpu.SemaphoreType.DMA((z.groups + 8,)),
         ],
         compiler_params=pltpu.CompilerParams(
             vmem_limit_bytes=VMEM_BYTES, collective_id=0, has_side_effects=True
@@ -699,8 +747,18 @@
             plant_capacity, plant_cost, store_capacity, store_cost,
         )
     ]
-    outs = run_step(z, block_pattern, big, small)
-    gen, chg, dis, plant, stored, balance, line, head, empty, full = outs[1:]
+    outs = run_step(z, block_pattern, big, small)[1:]
+    hbm = pl.BlockSpec(memory_space=pltpu.HBM)
+    gen, chg, dis, plant, stored, line, head, empty, full, balance = pl.pallas_call(
+        functools.partial(hand_on, len(outs)),
+        out_shape=[jax.ShapeDtypeStruct(x.shape, x.dtype) for x in outs],
+        in_specs=[hbm] * len(outs),
+        out_specs=[hbm] * len(outs),
+        scratch_shapes=[pltpu.VMEM(x.shape, x.dtype) for x in outs]
+        + [pltpu.SemaphoreType.DMA((len(outs),))] * 2,
+        compiler_params=pltpu.CompilerParams(vmem_limit_bytes=VMEM_BYTES),
+        name="results",
+    )(*outs)
     return (
         gen[None], chg[None], dis[None], plant[0], stored[0], balance,
         line[None], head[None], empty[None], full[None],

time: 326 us -> 287 us (0.88)
  Pallas kernels: 313 us -> 285 us
  local copies, waits for them, and re-layouts: 10.9 us -> 0 us
    pallas_call x1, Pallas kernels: 313 us -> 280 us  [run_step(): pl.pallas_call(functools.partial(step_kernel, z), out_shape=outs, in_spec...]
    unnamed x28 -> x0, local copies, waits for them, and re-layouts: 10.9 us -> none
    pallas_call x0 -> x1, Pallas kernels: none -> 5.1 us  [body(): pl.pallas_call(functools.partial(hand_on, len(outs)), out_shape=[jax.Shap...]
where the time goes in v2:
time: 287 us; the launch traced here: 285 us
  Pallas kernels  285 us (99%)
    pallas_call x1, Pallas kernels, run_step(): pl.pallas_call(functools.partial(step_kernel, z), out_shape=outs, in_spec...  280 us

profile of v2, /device:TPU:0, one launch (start us, length us, event | category | flops | bytes accessed | tf_op | source)
XLA Modules:
  0.0 285.4 jit_solution(9354161063690056584)
XLA Ops:
  0.7 279.6 %iteration.1 = (f32[4,16,256,640]{3,2,1,0:T(8,128)}, f32[168,2048]{1,0:T(8,128)}, f32[168,512]{1,0:T(8,128)}, f32[168,512]{1,0:T(8,128)}, f32[1,2048]{1,0:T(1,12...) custom-call(s32[8,10]{1,0:T(8,128)} %pat.1, ...), custom_call_target="tpu_custom_call" | custom-call | flops 21139292160 | bytes 125829120 | tf_op jit(solution)/shard_map/iteration/pallas_call | solution.py:678
  280.3 5.1 %results.1 = (f32[168,2048]{1,0:T(8,128)}, f32[168,512]{1,0:T(8,128)}, f32[168,512]{1,0:T(8,128)}, f32[1,2048]{1,0:T(1,128)}, f32[1,512]{1,0:T(1,128)}, /*index=...) custom-call(f32[168,2048]{1,0:T(8,128)} %get-tuple-element.30.refs_0_, ...), custom_call_target="tpu_custom_call" | custom-call | tf_op jit(solution)/shard_map/results/pallas_call | solution.py:752

commit v3 on v2

--- a/solution.py
+++ b/solution.py
@@ -132,7 +132,7 @@
         na, nb = self.z.a, self.z.b
         span = [0] + [s * k for k in range(1, na) for s in (-1, 1)]
         side = [0] + [s * k for k in range(1, nb) for s in (-1, 1)]
-        steps = [[] for _ in range(na)]
+        steps = [[] for _ in range(na + 1)]
         for t in range(na - 1):
             for s, way in ((-1, UP), (1, DOWN)):
                 steps[t].append((0, s * (t + 1), 0, [way, RIGHT, LEFT, CORE]))
@@ -142,11 +142,11 @@
         for t in range(na - 1):
             for e in side:
                 for s, way in ((-1, UP), (1, DOWN)):
-                    steps[min(na - 1, t + max(abs(e) - 1, 0))].append((1, s * (t + 1), e, [way, CORE]))
+                    steps[min(na, t + abs(e))].append((1, s * (t + 1), e, [way, CORE]))
         for u in range(nb - 1):
             for d in span:
                 for s, way in ((-1, RIGHT), (1, LEFT)):
-                    steps[min(na - 1, abs(d) + u)].append((0, d, s * (u + 1), [way, CORE]))
+                    steps[min(na, abs(d) + u + 1)].append((0, d, s * (u + 1), [way, CORE]))
         return steps
 
     def valid(self, d, e):
@@ -374,7 +374,7 @@
                     parts_r[g * (z.pairs + 1) + p] = r[:, p * LANES - c0 : (p + 1) * LANES - c0]
             return carry
 
-        lax.fori_loop(0, z.groups, group, 0)
+        lax.fori_loop(0, z.groups, group, 0, unroll=2)
 
     def collect(m):
         found = []
@@ -563,15 +563,16 @@
         for c in results[6:]:
             c.start()
 
-    steps = z.a
+    steps = z.a + 1
     points = 3
+    lead = 1
 
     def event(k, t):
-        q = k - t // points
+        q = k - t // points if t else k + lead
 
         def act():
             if t == 0:
-                pl.when(q > 0)(lambda: begin(q))
+                begin(q)
             else:
                 ga.step(q, t - 1)
             if t == steps:
@@ -602,7 +603,7 @@
 
     def make_flows(q):
         each(hold_in)
-        pl.loop(0, z.groups)(functools.partial(flow, q))
+        lax.fori_loop(0, z.groups, lambda g, c: (flow(q, g), c)[1], 0, unroll=2)
 
     tasks = [[] for _ in range(points)]
     for i, task in enumerate((make_image, make_dispatch, make_flows)):
@@ -619,7 +620,7 @@
                         if r < z.rounds:
                             sum_copy(r).start()
 
-            for t in range(o, steps + 1, points):
+            for t in reversed(range(o, steps + 1, points)):
                 event(k, t)
             if o == 0:
                 pl.when(k == 0)(prepare_sums)

time: 287 us -> 268 us (0.934)
  Pallas kernels: 285 us -> 265 us
    pallas_call x1, Pallas kernels: 280 us -> 260 us  [run_step(): pl.pallas_call(functools.partial(step_kernel, z), out_shape=outs, in_spec...]
where the time goes in v3:
time: 268 us; the launch traced here: 266 us
  Pallas kernels  265 us (99%)
    pallas_call x1, Pallas kernels, run_step(): pl.pallas_call(functools.partial(step_kernel, z), out_shape=outs, in_spec...  260 us

profile of v3, /device:TPU:0, one launch (start us, length us, event | category | flops | bytes accessed | tf_op | source)
XLA Modules:
  0.0 265.9 jit_solution(8389505993242796317)
XLA Ops:
  0.7 260.2 %iteration.1 = (f32[4,16,256,640]{3,2,1,0:T(8,128)}, f32[168,2048]{1,0:T(8,128)}, f32[168,512]{1,0:T(8,128)}, f32[168,512]{1,0:T(8,128)}, f32[1,2048]{1,0:T(1,12...) custom-call(s32[8,10]{1,0:T(8,128)} %pat.1, ...), custom_call_target="tpu_custom_call" | custom-call | flops 21139292160 | bytes 125829120 | tf_op jit(solution)/shard_map/iteration/pallas_call | solution.py:679
  260.8 5.1 %results.1 = (f32[168,2048]{1,0:T(8,128)}, f32[168,512]{1,0:T(8,128)}, f32[168,512]{1,0:T(8,128)}, f32[1,2048]{1,0:T(1,128)}, f32[1,512]{1,0:T(1,128)}, /*index=...) custom-call(f32[168,2048]{1,0:T(8,128)} %get-tuple-element.30.refs_0_, ...), custom_call_target="tpu_custom_call" | custom-call | tf_op jit(solution)/shard_map/results/pallas_call | solution.py:753
